TPU v7x, 32 devices: a whole 2x2x4 slice. The times are simulated.
32 devices in a mesh: wide: 8 (over z, x), narrow: 4 (over y, core).
Axes of the slice: x: 2, y: 2, z: 4, core: 2. Of those that a mesh axis runs over, the one named last changes fastest.
Arguments:
- density: bfloat16 [4096, 4096], P('wide', 'narrow'), may hold values from -0.0059814453 to 0.0059814453
- block_slot: int32 [32], replicated, may hold values from 0 to 31, as said below
- region_blocks: int32 [512], P(('wide', 'narrow')), may hold values from 0 to 31, as said below
- basis_lists: int32 [384, 8], P(('wide', 'narrow')), may hold values from 0 to 15, as said below
- point_counts: int32 [384], P(('wide', 'narrow')), may hold values from 1 to 256
- orbitals: bfloat16 [384, 1024, 256], P(('wide', 'narrow')), may hold values from -6 to 6
- weights: float32 [384, 256], P(('wide', 'narrow')), may hold values from 0.01 to 0.1
- harmonics: bfloat16 [384, 64, 256], P(('wide', 'narrow')), may hold values from -32 to 32
Outputs:
- hamiltonian: float32 [4096, 4096], P('wide', 'narrow')
Inputs may be any that keep to these rules, and one draw needn't show every extreme that they name: `block_slot`: a permutation of the 32 layout slots. `region_blocks`: the 16 blocks of one region are distinct; among the 256 block pairs of one region, no owner of the layout holds more than 8, and some owner holds exactly 8. `basis_lists`: the 8 positions of one list are distinct.
All inputs are finite; a program needn't handle non-finite values.
Results may differ from a plain program's by a relative error of at most 0.0023.
Values may be sent and summed in bfloat16 or wider, within the bound.
A program may use at most 128 MiB of HBM per device.

v0:
```python
import functools
import math

import jax
import jax.numpy as jnp
from jax import lax
from jax.experimental import pallas as pl
from jax.experimental.pallas import tpu as pltpu
from jax.sharding import PartitionSpec as P

BLK = 128
FAR_COEFF = 10.0
RING = 4
LANES = 128
MESH = pl.DeviceIdType.MESH
VMEM_BYTES = 58 * 1024 * 1024


def plane_peer(offset, inner, narrow):
    wide_me = lax.axis_index("wide")
    group = inner * narrow
    base = wide_me // inner * inner
    mine = wide_me % inner * narrow + lax.axis_index("narrow")
    other = lax.rem(mine + offset, group)
    return mine, other, (base + other // narrow, other % narrow)


def ring_device(shift, inner):
    wide = lax.axis_size("wide")
    return (lax.rem(lax.axis_index("wide") + shift * inner + wide, wide), lax.axis_index("narrow"))


def entry_barrier(steps, inner, narrow):
    barrier = pltpu.get_barrier_semaphore()
    group = inner * narrow

    def greet(offset, carry):
        _, _, device = plane_peer(offset, inner, narrow)
        pl.semaphore_signal(barrier, inc=1, device_id=device, device_id_type=MESH)
        return carry

    lax.fori_loop(1, group, greet, 0)
    if steps > 1:
        for shift in (1, -1):
            pl.semaphore_signal(
                barrier, inc=1, device_id=ring_device(shift, inner), device_id_type=MESH
            )
    pl.semaphore_wait(barrier, group - 1 + (2 if steps > 1 else 0))


def any_device(offset):
    narrow = lax.axis_size("narrow")
    devices = lax.axis_size("wide") * narrow
    mine = lax.axis_index("wide") * narrow + lax.axis_index("narrow")
    other = lax.rem(mine + offset, devices)
    return mine, (other // narrow, other % narrow)


def gather_kernel(
    steps,
    inner,
    narrow,
    row_cap,
    col_cap,
    lists_ref,
    row_ref,
    col_ref,
    counts_ref,
    tile_ref,
    weights_ref,
    dens_ref,
    orb_ref,
    harm_ref,
    tables_ref,
    rho_ref,
    total_ref,
    *rest,
):
    arrived, rest = rest[0], rest[1:]
    raws, rest = rest[:steps], rest[steps:]
    (
        chosen,
        table,
        orbs,
        harms,
        matrix,
        moment,
        share,
        shares,
        send_sem,
        recv_sem,
        ring_send,
        ring_recv,
        own_sem,
        load_sem,
        tile_send,
        tile_recv,
        local_sem,
        share_send,
        share_recv,
    ) = rest
    devices = lax.axis_size("wide") * narrow
    inner_me = lax.axis_index("wide") % inner
    narrow_me = lax.axis_index("narrow")
    cap = row_cap * col_cap
    group = inner * narrow
    ring_me = lax.axis_index("wide") // inner
    mine, _, _ = plane_peer(0, inner, narrow)
    col_blocks = dens_ref.shape[1] // BLK
    held = raws[0].shape[0]
    half = held // 2

    def load_copy(place):
        row, col = place // col_blocks, place % col_blocks
        return pltpu.make_async_copy(
            dens_ref.at[
                pl.ds(pl.multiple_of(row * BLK, BLK), BLK),
                pl.ds(pl.multiple_of(col * BLK, BLK), BLK),
            ],
            raws[0].at[place],
            load_sem.at[place],
        )

    def load(place, carry):
        load_copy(place).start()
        return carry

    def loaded(place, carry):
        load_copy(place).wait()
        return carry

    def pick(step):
        ring = lax.rem(ring_me - step + steps, steps)

        def body(offset, carry):
            _, other, _ = plane_peer(offset, inner, narrow)
            for rr in range(row_cap):
                row = table[other, 0, (ring * inner + inner_me) * row_cap + rr] * col_blocks
                for cr in range(col_cap):
                    place = row + table[other, 1, narrow_me * col_cap + cr]
                    chosen[step, offset, rr * col_cap + cr] = raws[step][place]
            return carry

        lax.fori_loop(0, group, body, 0)

    def block_copy(step, offset):
        _, _, device = plane_peer(offset, inner, narrow)
        return pltpu.make_async_remote_copy(
            src_ref=chosen.at[step, offset],
            dst_ref=arrived.at[pl.ds((step * group + mine) * cap, cap)],
            send_sem=send_sem.at[step, offset - 1],
            recv_sem=recv_sem.at[step, offset - 1],
            device_id=device,
            device_id_type=MESH,
        )

    def ring_copy(step, piece):
        span = pl.ds(piece * half, half)
        return pltpu.make_async_remote_copy(
            src_ref=raws[step].at[span],
            dst_ref=raws[step + 1].at[span],
            send_sem=ring_send.at[step, piece],
            recv_sem=ring_recv.at[step, piece],
            device_id=ring_device(1, inner),
            device_id_type=MESH,
        )

    def own_copy(step):
        return pltpu.make_async_copy(
            chosen.at[step, 0],
            arrived.at[pl.ds((step * group + mine) * cap, cap)],
            own_sem.at[step],
        )

    def tile_copy(offset):
        _, _, device = plane_peer(offset, inner, narrow)
        return pltpu.make_async_remote_copy(
            src_ref=tile_ref,
            dst_ref=tables_ref.at[mine],
            send_sem=tile_send.at[offset - 1],
            recv_sem=tile_recv.at[offset - 1],
            device_id=device,
            device_id_type=MESH,
        )

    def share_copy(offset):
        whose, device = any_device(offset)
        return pltpu.make_async_remote_copy(
            src_ref=share,
            dst_ref=shares.at[whose],
            send_sem=share_send.at[offset - 1],
            recv_sem=share_recv.at[offset - 1],
            device_id=device,
            device_id_type=MESH,
        )

    def over(count, make, act):
        def body(offset, carry):
            act(make(offset))
            return carry

        lax.fori_loop(1, count, body, 0)

    start = lambda copy: copy.start()
    wait = lambda copy: copy.wait()

    load_orbs = pltpu.make_async_copy(orb_ref, orbs, local_sem.at[0])
    load_harms = pltpu.make_async_copy(harm_ref, harms, local_sem.at[1])
    for step in range(steps):
        if step == 0:
            tables_ref[mine] = tile_ref[...]
            lax.fori_loop(0, held, load, 0)
            barrier = pltpu.get_barrier_semaphore()

            def greet(offset, carry):
                _, device = any_device(offset)
                pl.semaphore_signal(barrier, inc=1, device_id=device, device_id_type=MESH)
                return carry

            lax.fori_loop(1, devices, greet, 0)
            load_orbs.start()
            load_harms.start()
            lax.fori_loop(0, held, loaded, 0)
            pl.semaphore_wait(barrier, devices - 1)
            over(group, tile_copy, start)
        for piece in range(2):
            if step > 0:
                ring_copy(step - 1, piece).wait_recv()
            if step < steps - 1:
                ring_copy(step, piece).start()
        if step == 0:
            over(group, tile_copy, wait)
            to_table = pltpu.make_async_copy(tables_ref, table, local_sem.at[2])
            to_table.start()
            to_table.wait()
        pick(step)

        def send(offset, carry, step=step):
            block_copy(step, offset).start()
            return carry

        lax.fori_loop(1, group, send, 0)
        own_copy(step).start()
    for step in range(steps):

        def finish(offset, carry, step=step):
            block_copy(step, offset).wait()
            return carry

        lax.fori_loop(1, group, finish, 0)
        own_copy(step).wait()
        if step < steps - 1:
            for piece in range(2):
                ring_copy(step, piece).wait_send()
    load_orbs.wait()
    load_harms.wait()

    list_len = lists_ref.shape[1]
    height, points = orbs.shape[1:]
    each = 2 * BLK
    moment[...] = jnp.zeros_like(moment)

    def add_batch(batch, carry):
        places = [lists_ref[batch, k] for k in range(list_len)]
        cols = [col_ref[place] for place in places]
        for k in range(list_len):
            row = row_ref[places[k]]
            for k2 in range(list_len):
                spot = row + cols[k2]
                matrix[k * BLK : (k + 1) * BLK, k2 * BLK : (k2 + 1) * BLK] = arrived[spot]
        total = jnp.zeros((1, points), jnp.float32)
        for top in range(0, height, each):
            product = jnp.dot(
                matrix[top : top + each, :], orbs[batch], preferred_element_type=jnp.float32
            )
            part = product * orbs[batch, top : top + each, :].astype(jnp.float32)
            total += jnp.sum(part, axis=0, keepdims=True)
        rho_ref[pl.ds(batch, 1), :] = total
        live = live_row(weights_ref, counts_ref, batch) * total
        moment[...] += harms[batch].astype(jnp.float32) * live
        return carry

    lax.fori_loop(0, orbs.shape[0], add_batch, 0)
    components = moment.shape[0]
    diagonal = lax.broadcasted_iota(jnp.int32, (components, LANES), 0) == lax.broadcasted_iota(
        jnp.int32, (components, LANES), 1
    )
    summed = jnp.sum(moment[...], axis=1, keepdims=True)
    line = jnp.sum(jnp.where(diagonal, summed, 0.0), axis=0, keepdims=True)
    share[...] = jnp.broadcast_to(line, share.shape)
    whose, _ = any_device(0)
    shares[whose] = jnp.broadcast_to(line, share.shape)
    over(devices, share_copy, start)
    over(devices, share_copy, wait)
    line = jnp.sum(shares[...], axis=0)[0:1]
    total_ref[...] = jnp.sum(jnp.where(diagonal, line, 0.0), axis=1, keepdims=True)


def gather_density(
    lists, rows, cols, counts, tile, weights, dens, orbitals, harmonics, steps, inner, narrow, caps
):
    row_cap, col_cap = caps
    group = inner * narrow
    cap = row_cap * col_cap
    devices = steps * group
    ring_sems = max(1, steps - 1)
    held = dens.shape[0] // BLK * (dens.shape[1] // BLK)
    batches, height, points = orbitals.shape
    components = harmonics.shape[1]
    vmem = pl.BlockSpec(memory_space=pltpu.VMEM)
    smem = pl.BlockSpec(memory_space=pltpu.SMEM)
    anywhere = pl.BlockSpec(memory_space=pl.ANY)
    return pl.pallas_call(
        functools.partial(gather_kernel, steps, inner, narrow, row_cap, col_cap),
        out_shape=[
            jax.ShapeDtypeStruct((group,) + tile.shape, tile.dtype),
            jax.ShapeDtypeStruct((batches, points), jnp.float32),
            jax.ShapeDtypeStruct((components, 1), jnp.float32),
        ],
        in_specs=[smem] * 4 + [vmem] * 2 + [anywhere] * 3,
        out_specs=[vmem] * 3,
        scratch_shapes=[pltpu.VMEM((steps * group * cap, BLK, BLK), dens.dtype)]
        + [pltpu.VMEM((held, BLK, BLK), dens.dtype)] * steps
        + [
            pltpu.VMEM((steps, group, cap, BLK, BLK), dens.dtype),
            pltpu.SMEM((group,) + tile.shape, tile.dtype),
            pltpu.VMEM(orbitals.shape, orbitals.dtype),
            pltpu.VMEM(harmonics.shape, harmonics.dtype),
            pltpu.VMEM((height, height), dens.dtype),
            pltpu.VMEM((components, points), jnp.float32),
            pltpu.VMEM((8, LANES), jnp.float32),
            pltpu.VMEM((devices, 8, LANES), jnp.float32),
            pltpu.SemaphoreType.DMA((steps, group - 1)),
            pltpu.SemaphoreType.DMA((steps, group - 1)),
            pltpu.SemaphoreType.DMA((ring_sems, 2)),
            pltpu.SemaphoreType.DMA((ring_sems, 2)),
            pltpu.SemaphoreType.DMA((steps,)),
            pltpu.SemaphoreType.DMA((held,)),
            pltpu.SemaphoreType.DMA((group - 1,)),
            pltpu.SemaphoreType.DMA((group - 1,)),
            pltpu.SemaphoreType.DMA((3,)),
            pltpu.SemaphoreType.DMA((devices - 1,)),
            pltpu.SemaphoreType.DMA((devices - 1,)),
        ],
        compiler_params=pltpu.CompilerParams(
            collective_id=1, has_side_effects=True, vmem_limit_bytes=63 * 1024 * 1024
        ),
        name="gather_density",
    )(lists, rows, cols, counts, tile, weights, dens, orbitals, harmonics)


def return_kernel(steps, inner, narrow, cap, table_ref, *rest):
    parts, rest = rest[:steps], rest[steps:]
    out_ref, rest = rest[0], rest[1:]
    gots, rest = rest[:steps], rest[steps:]
    runs, rest = rest[: steps - 1], rest[steps - 1 :]
    prevs, rest = (None,) + rest[: steps - 1], rest[steps - 1 :]
    send_sem, recv_sem, ring_send, ring_recv, own_sem = rest
    group = inner * narrow
    ring_me = lax.axis_index("wide") // inner
    mine, _, _ = plane_peer(0, inner, narrow)
    row_blocks = out_ref.shape[0] // BLK
    col_blocks = out_ref.shape[1] // BLK
    empty = group * cap
    inner_me = lax.axis_index("wide") % inner
    narrow_me = lax.axis_index("narrow")

    def block_copy(step, offset):
        _, other, device = plane_peer(offset, inner, narrow)
        return pltpu.make_async_remote_copy(
            src_ref=parts[step].at[pl.ds(other * cap, cap)],
            dst_ref=gots[step].at[pl.ds(mine * cap, cap)],
            send_sem=send_sem.at[step, offset - 1],
            recv_sem=recv_sem.at[step, offset - 1],
            device_id=device,
            device_id_type=MESH,
        )

    def own_copy(step):
        span = pl.ds(mine * cap, cap)
        return pltpu.make_async_copy(parts[step].at[span], gots[step].at[span], own_sem.at[step])

    def ring_copy(step, piece):
        span = pl.ds(piece * BLK, BLK)
        return pltpu.make_async_remote_copy(
            src_ref=runs[step].at[span],
            dst_ref=prevs[step + 1].at[span],
            send_sem=ring_send.at[step, piece],
            recv_sem=ring_recv.at[step, piece],
            device_id=ring_device(1, inner),
            device_id_type=MESH,
        )

    def start_step(step):
        own_copy(step).start()

        def send(offset, carry):
            block_copy(step, offset).start()
            return carry

        lax.fori_loop(1, group, send, 0)

    for step in range(steps):
        gots[step][empty] = jnp.zeros((BLK, BLK), gots[step].dtype)
    entry_barrier(steps, inner, narrow)
    for step in range(min(2, steps)):
        start_step(step)
    for step in range(steps):
        last = step == steps - 1
        ring = lax.rem(ring_me - 1 - step + 2 * steps, steps)

        def arrive(offset, carry, step=step):
            block_copy(step, offset).wait_recv()
            return carry

        lax.fori_loop(1, group, arrive, 0)
        own_copy(step).wait()
        if step + 2 < steps:
            start_step(step + 2)

        def add_row(piece, carry, step=step, last=last, ring=ring):
            if step > 0:
                ring_copy(step - 1, piece).wait_recv()
            span = pl.ds(pl.multiple_of(piece * BLK, BLK), BLK)
            bases = [
                table_ref[source, 2, (ring * inner + inner_me) * row_blocks + piece] + source * cap
                for source in range(group)
            ]

            def add_block(block, inner_carry):
                across = pl.ds(pl.multiple_of(block * BLK, BLK), BLK)
                if step > 0:
                    total = prevs[step][span, across].astype(jnp.float32)
                else:
                    total = jnp.zeros((BLK, BLK), jnp.float32)
                for source in range(group):
                    col = table_ref[source, 3, narrow_me * col_blocks + block]
                    place = jnp.minimum(bases[source] + col, empty)
                    total += gots[step][place].astype(jnp.float32)
                if last:
                    out_ref[span, across] = total
                else:
                    runs[step][span, across] = total.astype(runs[step].dtype)
                return inner_carry

            lax.fori_loop(0, col_blocks, add_block, 0)
            if not last:

                @pl.when(piece > 0)
                def _():
                    ring_copy(step, piece - 1).start()

            return carry

        lax.fori_loop(0, row_blocks, add_row, 0)
        if not last:
            ring_copy(step, row_blocks - 1).start()
    for step in range(steps):

        def finish(offset, carry, step=step):
            block_copy(step, offset).wait_send()
            return carry

        lax.fori_loop(1, group, finish, 0)
        if step < steps - 1:

            def left(piece, carry, step=step):
                ring_copy(step, piece).wait_send()
                return carry

            lax.fori_loop(0, row_blocks, left, 0)


def return_blocks(parts, tables, shape, steps, inner, narrow, cap):
    group = inner * narrow
    ring_sems = max(1, steps - 1)
    row_blocks = shape[0] // BLK
    dtype = parts[0].dtype
    return pl.pallas_call(
        functools.partial(return_kernel, steps, inner, narrow, cap),
        out_shape=jax.ShapeDtypeStruct(shape, jnp.float32),
        in_specs=[pl.BlockSpec(memory_space=pltpu.SMEM)]
        + [pl.BlockSpec(memory_space=pl.ANY)] * steps,
        out_specs=pl.BlockSpec(memory_space=pltpu.VMEM),
        scratch_shapes=[pltpu.VMEM((group * cap + 1, BLK, BLK), dtype)] * steps
        + [pltpu.VMEM(shape, dtype)] * (2 * (steps - 1))
        + [
            pltpu.SemaphoreType.DMA((steps, group - 1)),
            pltpu.SemaphoreType.DMA((steps, group - 1)),
            pltpu.SemaphoreType.DMA((ring_sems, row_blocks)),
            pltpu.SemaphoreType.DMA((ring_sems, row_blocks)),
            pltpu.SemaphoreType.DMA((steps,)),
        ],
        compiler_params=pltpu.CompilerParams(
            collective_id=3, has_side_effects=True, vmem_limit_bytes=VMEM_BYTES
        ),
        name="return_blocks",
    )(tables, *parts)


def live_row(weights_ref, counts_ref, batch):
    points = weights_ref.shape[1]
    point = lax.broadcasted_iota(jnp.int32, (1, points), 1)
    return jnp.where(
        point < counts_ref[batch], weights_ref[pl.ds(batch, 1), :], jnp.float32(0.0)
    )


def integral_kernel(
    steps,
    list_len,
    far_scale,
    lists_ref,
    row_ref,
    col_ref,
    counts_ref,
    orb_ref,
    harm_ref,
    weights_ref,
    rho_ref,
    moment_ref,
    *rest,
):
    outs = rest[:steps]
    acc, stage, sems = rest[steps:]
    batch = pl.program_id(0)
    per_chunk = acc.shape[0] // steps

    @pl.when(batch == 0)
    def _():
        @pl.loop(0, acc.shape[0])
        def _(place):
            acc[place] = jnp.zeros(acc.shape[1:], jnp.float32)

    rho = rho_ref[pl.ds(batch, 1), :]
    far = FAR_COEFF * jnp.sum(
        moment_ref[...] * harm_ref[0].astype(jnp.float32), axis=0, keepdims=True
    )
    sixth = jnp.exp(jnp.log(1.0 + rho * rho) * (1.0 / 6.0))
    potential = 0.5 * rho - sixth + far / far_scale
    factor = live_row(weights_ref, counts_ref, batch) * potential
    orbs = orb_ref[0]
    scaled = (orbs.astype(jnp.float32) * factor).astype(jnp.bfloat16)
    places = [lists_ref[batch, k] for k in range(list_len)]
    rows = [row_ref[place] for place in places]
    cols = [col_ref[place] for place in places]
    for pair in range(0, list_len, 2):
        right = orb_ref[0, pair * BLK : (pair + 2) * BLK, :]
        term = lax.dot_general(
            scaled, right, (((1,), (1,)), ((), ())), preferred_element_type=jnp.float32
        )
        for k in range(list_len):
            for k2 in range(2):
                acc[rows[k] + cols[pair + k2]] += term[
                    k * BLK : (k + 1) * BLK, k2 * BLK : (k2 + 1) * BLK
                ]

    @pl.when(batch == pl.num_programs(0) - 1)
    def _():
        copies = []
        for k in range(steps):
            if k >= 2:
                copies[k - 2].wait()

            @pl.loop(0, per_chunk)
            def _(place, k=k):
                stage[k % 2, place] = acc[k * per_chunk + place].astype(jnp.bfloat16)

            copy = pltpu.make_async_copy(stage.at[k % 2], outs[k], sems.at[k])
            copy.start()
            copies.append(copy)
        for copy in copies[-2:]:
            copy.wait()


def integrals(lists, rows, cols, counts, orbitals, harmonics, weights, rho, moments, steps, held, far_scale):
    batches, height, points = orbitals.shape
    list_len = lists.shape[1]
    components = harmonics.shape[1]
    per_chunk = held // steps
    full = lambda shape: pl.BlockSpec(shape, lambda g, *_: (0, 0))
    return pl.pallas_call(
        functools.partial(integral_kernel, steps, list_len, far_scale),
        out_shape=[jax.ShapeDtypeStruct((per_chunk, BLK, BLK), jnp.bfloat16)] * steps,
        grid_spec=pltpu.PrefetchScalarGridSpec(
            num_scalar_prefetch=4,
            grid=(batches,),
            in_specs=[
                pl.BlockSpec((1, height, points), lambda g, *_: (g, 0, 0)),
                pl.BlockSpec((1, components, points), lambda g, *_: (g, 0, 0)),
                full((batches, points)),
                full((batches, points)),
                full((components, 1)),
            ],
            out_specs=[pl.BlockSpec(memory_space=pl.ANY)] * steps,
            scratch_shapes=[
                pltpu.VMEM((held, BLK, BLK), jnp.float32),
                pltpu.VMEM((2, per_chunk, BLK, BLK), jnp.bfloat16),
                pltpu.SemaphoreType.DMA((steps,)),
            ],
        ),
        compiler_params=pltpu.CompilerParams(vmem_limit_bytes=VMEM_BYTES),
        name="integrals",
    )(lists, rows, cols, counts, orbitals, harmonics, weights, rho, moments)


def rank_among(keys):
    count = keys.shape[0]
    order = jnp.arange(count)
    same = (keys[:, None] == keys[None, :]) & (order[None, :] < order[:, None])
    return jnp.sum(same.astype(jnp.int32), axis=1)


def spread(positions, values, size):
    hit = positions[None, :] == jnp.arange(size)[:, None]
    return jnp.sum(jnp.where(hit, values[None, :], 0), axis=1)


def per_device(
    region, density, block_slot, region_blocks, basis_lists, point_counts, orbitals, weights, harmonics
):
    wide = lax.axis_size("wide")
    narrow = lax.axis_size("narrow")
    devices = wide * narrow
    steps = math.gcd(wide, RING)
    inner = wide // steps
    group = inner * narrow
    row_cap = max(1, region // wide)
    col_cap = region // narrow
    cap = row_cap * col_cap
    wide_me = lax.axis_index("wide")
    ring_me = wide_me // inner

    known = block_slot.shape[0]
    hit = region_blocks[:, None] == jnp.arange(known)[None, :]
    slots = jnp.sum(jnp.where(hit, block_slot[None, :], 0), axis=1)
    row_owner, row_local = slots % wide, slots // wide
    col_owner, col_local = slots % narrow, slots // narrow
    row_rank, col_rank = rank_among(row_owner), rank_among(col_owner)
    row_table = spread(row_owner * row_cap + row_rank, row_local, LANES)
    col_table = spread(col_owner * col_cap + col_rank, col_local, LANES)
    far = 1 << 20
    row_blocks = density.shape[0] // BLK
    col_blocks = density.shape[1] // BLK
    row_back = far + spread(
        row_owner * row_blocks + row_local, row_rank * col_cap - far, LANES
    )
    col_back = far + spread(col_owner * col_blocks + col_local, col_rank - far, LANES)
    tile = jnp.stack([row_table, col_table, row_back, col_back] * 2)
    col_place = col_owner * cap + col_rank
    in_plane = row_owner % inner * (narrow * cap) + row_rank * col_cap
    owner_ring = row_owner // inner
    row_in = (ring_me - owner_ring + steps) % steps * (group * cap) + in_plane
    row_out = (ring_me - 1 - owner_ring + 2 * steps) % steps * (group * cap) + in_plane

    tables, rho, moments = gather_density(
        basis_lists,
        row_in,
        col_place,
        point_counts,
        tile,
        weights,
        density,
        orbitals,
        harmonics,
        steps,
        inner,
        narrow,
        (row_cap, col_cap),
    )
    components = harmonics.shape[1]
    total_points = orbitals.shape[0] * orbitals.shape[2] * devices
    parts = integrals(
        basis_lists,
        row_out,
        col_place,
        point_counts,
        orbitals,
        harmonics,
        weights,
        rho,
        moments,
        steps,
        steps * group * cap,
        math.sqrt(total_points * components),
    )
    return return_blocks(
        parts,
        tables,
        density.shape,
        steps,
        inner,
        narrow,
        cap,
    )


def solution(mesh):
    devices = mesh.shape["wide"] * mesh.shape["narrow"]

    def whole(density, block_slot, region_blocks, *others):
        region = region_blocks.shape[0] // devices
        in_specs = (
            P("wide", "narrow"),
            P(),
            P(("wide", "narrow")),
            P(("wide", "narrow"), None),
            P(("wide", "narrow")),
            P(("wide", "narrow"), None, None),
            P(("wide", "narrow"), None),
            P(("wide", "narrow"), None, None),
        )
        mapped = jax.shard_map(
            functools.partial(per_device, region),
            mesh=mesh,
            in_specs=in_specs,
            out_specs=P("wide", "narrow"),
            check_vma=False,
        )
        return mapped(density, block_slot, region_blocks, *others)

    return whole
```

profile of v0, /device:TPU:0, one launch (start us, length us, event | category | flops | bytes accessed | tf_op | source)
XLA Modules:
  0.0 245.0 jit_solution(2188989772643438343)
XLA Ops:
  0.0 0.9 select_reduce_fusion.4
  0.9 0.2 convert_reduce_fusion
  1.1 0.2 convert_reduce_fusion.1
  1.2 0.6 multiply_add_fusion.1
  1.8 0.5 fusion.7
  2.4 0.1 select_reduce_fusion
  2.5 0.1 select_reduce_fusion.2
  2.5 0.6 fusion.3.row_ref
  3.1 0.6 stack.8.tile_ref
  3.8 1.4 copy.11.lists_ref
  5.1 120.2 %gather_density.1 = (s32[8,8,128]{2,1,0:T(8,128)}, f32[12,256]{1,0:T(8,128)}, f32[64,1]{1,0:T(8,128)}) custom-call(s32[12,8]{1,0:T(8,128)} %copy.11.lists_ref, s32[16]{0:T(128)} %fusion.3.row_ref, s32[16]{0:T(128)} %get-tuple-element.29.col_ref, s32[12]{0:T(128)} %counts_ref.3, s32[8,128]{1,0:T(8,128)} %stack.8.tile_ref, f32[12,256]{1,0:T(8,128)} %weights_ref.3, ...), custom_call_target="tpu_custom_call" | custom-call | tf_op jit(solution)/shard_map/gather_density/pallas_call | solution.py:313
  125.3 19.6 %integrals.1 = (bf16[64,128,128]{2,1,0:T(8,128)(2,1)}, bf16[64,128,128]{2,1,0:T(8,128)(2,1)}, bf16[64,128,128]{2,1,0:T(8,128)(2,1)}, bf16[64,128,128]{2,1,0:T(8,128)(2,1)}) custom-call(s32[12,8]{1,0:T(8,128)} %copy.11.lists_ref, s32[16]{0:T(128)} %get-tuple-element.19.row_ref, s32[16]{0:T(128)} %get-tuple-element.29.col_ref, s32[12]{0:T(128)} %counts_ref.3, ...), custom_call_target="tpu_custom_call" | custom-call | tf_op jit(solution)/shard_map/integrals/pallas_call | solution.py:582
  144.9 97.0 %return_blocks.1 = f32[512,1024]{1,0:T(8,128)} custom-call(s32[8,8,128]{2,1,0:T(8,128)} %get-tuple-element.12.table_ref, bf16[64,128,128]{2,1,0:T(8,128)(2,1)} %get-tuple-element.15.rest_0_, bf16[64,128,128]{2,1,0:T(8,128)(2,1)} %get-tuple-element.16.rest_1_, bf16[64,128,128]{2,1,0:T(8,128)(2,1)} %get-tuple-element.17.rest_2_, ...), custom_call_target="tpu_custom_call" | custom-call | tf_op jit(solution)/shard_map/return_blocks/pallas_call | solution.py:479
  241.9 3.2 %copy.14 = f32[512,1024]{1,0:T(8,128)} copy(f32[512,1024]{1,0:T(8,128)} %return_blocks.1) | data formatting | bytes 4194304
  (3 shorter events, 0.0 us)
where the time goes:
time: 248 us; the launch traced here: 245 us
  Pallas kernels  237 us (96%)
  local copies, waits for them, and re-layouts  5.13 us (2%)
  other arithmetic  3.12 us (1%)
    pallas_call x1, Pallas kernels, gather_density(): pl.pallas_call(functools.partial(gather_kernel, steps, inner, narrow, row...  120 us
    pallas_call x1, Pallas kernels, return_blocks(): pl.pallas_call(functools.partial(return_kernel, steps, inner, narrow, cap...  97 us
    pallas_call x1, Pallas kernels, integrals(): pl.pallas_call(functools.partial(integral_kernel, steps, list_len, far_sc...  19.6 us

commit v1 on v0

v1 whole, which is shorter than its diff:
```python
import functools
import math

import jax
import jax.numpy as jnp
from jax import lax
from jax.experimental import pallas as pl
from jax.experimental.pallas import tpu as pltpu
from jax.sharding import PartitionSpec as P

BLK = 128
FAR_COEFF = 10.0
RING = 4
LANES = 128
CHUNK = 512
MESH = pl.DeviceIdType.MESH
VMEM_BYTES = 63 * 1024 * 1024


def ring_device(shift, inner):
    wide = lax.axis_size("wide")
    return (lax.rem(lax.axis_index("wide") + shift * inner + wide, wide), lax.axis_index("narrow"))


def any_device(offset):
    narrow = lax.axis_size("narrow")
    devices = lax.axis_size("wide") * narrow
    mine = lax.axis_index("wide") * narrow + lax.axis_index("narrow")
    other = lax.rem(mine + offset, devices)
    return mine, (other // narrow, other % narrow)


def step_kernel(
    steps,
    inner,
    narrow,
    row_cap,
    col_cap,
    far_scale,
    inv_ref,
    cols_ref,
    counts_ref,
    tile_ref,
    weights_ref,
    dens_ref,
    orb_ref,
    harm_ref,
    out_ref,
    *rest,
):
    raws, rest = rest[:steps], rest[steps:]
    arrs, rest = rest[:steps], rest[steps:]
    (
        chosen,
        tables,
        table,
        even,
        odd,
        phi,
        rows,
        harms,
        rho,
        factor,
        share,
        shares,
        ostage,
        send_sem,
        recv_sem,
        ring_send,
        ring_recv,
        load_sem,
        tile_send,
        tile_recv,
        orb_sem,
        local_sem,
        share_send,
        share_recv,
        out_sem,
    ) = rest
    devices = lax.axis_size("wide") * narrow
    group = inner * narrow
    cap = row_cap * col_cap
    wide_me = lax.axis_index("wide")
    inner_me = wide_me % inner
    ring_me = wide_me // inner
    base = ring_me * inner
    narrow_me = lax.axis_index("narrow")
    mine = inner_me * narrow + narrow_me
    col_blocks = dens_ref.shape[1] // BLK
    row_blocks = dens_ref.shape[0] // BLK
    held = row_blocks * col_blocks
    empty = group * cap
    batches, list_len, _, points = orb_ref.shape
    all_points = batches * points
    slots = narrow * col_cap
    tall = row_cap * BLK
    broad = col_cap * BLK

    def target(place):
        across = lax.rem(inner_me + place // narrow, inner)
        along = lax.rem(narrow_me + place % narrow, narrow)
        return across, along

    def source(place):
        across = lax.rem(inner_me + inner - place // narrow, inner)
        along = lax.rem(narrow_me + narrow - place % narrow, narrow)
        return across, along

    def load_copy(place):
        row, col = place // col_blocks, place % col_blocks
        return pltpu.make_async_copy(
            dens_ref.at[
                pl.ds(pl.multiple_of(row * BLK, BLK), BLK),
                pl.ds(pl.multiple_of(col * BLK, BLK), BLK),
            ],
            raws[0].at[place],
            load_sem.at[place],
        )

    stages = (even, odd)

    def orb_copy(batch, which):
        return pltpu.make_async_copy(
            orb_ref.at[batch], stages[which].at[pl.ds(0, list_len)], orb_sem.at[which]
        )

    def block_copy(step, place):
        across, along = target(place)
        return pltpu.make_async_remote_copy(
            src_ref=chosen.at[step % 2, place],
            dst_ref=arrs[step].at[pl.ds(mine * cap, cap)],
            send_sem=send_sem.at[step, place],
            recv_sem=recv_sem.at[step, place],
            device_id=(base + across, along),
            device_id_type=MESH,
        )

    def ring_copy(step, piece):
        span = pl.ds(piece * col_blocks, col_blocks)
        return pltpu.make_async_remote_copy(
            src_ref=raws[step].at[span],
            dst_ref=raws[step + 1].at[span],
            send_sem=ring_send.at[step, piece],
            recv_sem=ring_recv.at[step, piece],
            device_id=ring_device(1, inner),
            device_id_type=MESH,
        )

    def tile_copy(place):
        across, along = target(place)
        return pltpu.make_async_remote_copy(
            src_ref=tile_ref,
            dst_ref=tables.at[mine],
            send_sem=tile_send.at[place],
            recv_sem=tile_recv.at[place],
            device_id=(base + across, along),
            device_id_type=MESH,
        )

    def share_copy(offset):
        whose, device = any_device(offset)
        return pltpu.make_async_remote_copy(
            src_ref=share,
            dst_ref=shares.at[whose],
            send_sem=share_send.at[offset],
            recv_sem=share_recv.at[offset],
            device_id=device,
            device_id_type=MESH,
        )

    def over(first, last, make, act):
        def body(index, carry):
            act(make(index))
            return carry

        lax.fori_loop(first, last, body, 0)

    start = lambda copy: copy.start()
    wait = lambda copy: copy.wait()
    wait_send = lambda copy: copy.wait_send()
    wait_recv = lambda copy: copy.wait_recv()

    over(0, held, load_copy, start)
    barrier = pltpu.get_barrier_semaphore()

    def greet(offset, carry):
        _, device = any_device(offset)
        pl.semaphore_signal(barrier, inc=1, device_id=device, device_id_type=MESH)
        return carry

    lax.fori_loop(1, devices, greet, 0)
    for which in range(min(2, batches)):
        orb_copy(which, which).start()
    load_harms = pltpu.make_async_copy(harm_ref, harms, local_sem.at[0])
    load_harms.start()
    tables[mine] = tile_ref[...]
    for step in range(steps):
        arrs[step][empty] = jnp.zeros((BLK, BLK), arrs[step].dtype)
    for stage in stages:
        stage[list_len] = jnp.zeros((BLK, points), stage.dtype)
    phi[slots] = jnp.zeros((BLK, all_points), phi.dtype)
    rho[...] = jnp.zeros_like(rho)
    over(0, held, load_copy, wait)
    pl.semaphore_wait(barrier, devices - 1)
    over(1, group, tile_copy, start)

    def pass_on(step):
        for piece in range(row_blocks):
            if step > 0:
                ring_copy(step - 1, piece).wait_recv()
            if step < steps - 1:
                ring_copy(step, piece).start()

    def pick(step, place, put):
        across, along = target(place)
        other = across * narrow + along
        ring = lax.rem(ring_me - step + steps, steps)
        for rr in range(row_cap):
            row = table[other, 0, (ring * inner + inner_me) * row_cap + rr] * col_blocks
            for cr in range(col_cap):
                spot = row + table[other, 1, narrow_me * col_cap + cr]
                put(rr * col_cap + cr, raws[step][spot])

    def send_picks(step):
        def put_own(index, value):
            arrs[step][mine * cap + index] = value

        def body(count, carry):
            place = group - 1 - count

            def put(index, value):
                chosen[step % 2, place, index] = value

            pick(step, place, put)

            @pl.when(count > 0)
            def _():
                block_copy(step, place + 1).start()

            return carry

        lax.fori_loop(0, group - 1, body, 0)
        pick(step, 0, put_own)
        block_copy(step, 1).start()

    def density_piece(step, place):
        across, along = source(place)
        first = (across * narrow + along) * cap
        ring = lax.rem(ring_me - step + steps, steps)
        owner = (ring * inner + across) * row_cap
        block = jnp.concatenate(
            [
                jnp.concatenate(
                    [arrs[step][first + rr * col_cap + cr] for cr in range(col_cap)], axis=1
                )
                for rr in range(row_cap)
            ],
            axis=0,
        )
        spots = [cols_ref[owner + rr] for rr in range(row_cap)]
        down = pl.ds(along * col_cap, col_cap)

        def chunk(index, carry):
            span = pl.ds(pl.multiple_of(index * CHUNK, CHUNK), CHUNK)
            wave = phi[down, :, span].reshape(broad, CHUNK)
            product = jnp.dot(block, wave, preferred_element_type=jnp.float32)
            total = rho[:, span]
            for rr in range(row_cap):
                mate = phi[spots[rr], :, span]
                part = product[rr * BLK : (rr + 1) * BLK] * mate.astype(jnp.float32)
                total += jnp.sum(part.reshape(BLK // 8, 8, CHUNK), axis=0)
            rho[:, span] = total
            return carry

        lax.fori_loop(0, all_points // CHUNK, chunk, 0)

    def density_step(step):
        density_piece(step, 0)

        def body(count, carry):
            place = group - 1 - count
            block_copy(step, place).wait_recv()
            density_piece(step, place)
            return carry

        lax.fori_loop(0, group - 1, body, 0)

    def build(batch, which):
        orb_copy(batch, which).wait()
        across = pl.ds(pl.multiple_of(batch * points, points), points)
        for slot in range(slots):
            phi[slot, :, across] = stages[which][inv_ref[batch, slot]]

        @pl.when(batch + 2 < batches)
        def _():
            orb_copy(batch + 2, which).start()

    def build_pair(pair, carry):
        for which in range(2):
            build(pair * 2 + which, which)
        return carry

    pass_on(0)
    over(1, group, tile_copy, wait)
    to_table = pltpu.make_async_copy(tables, table, local_sem.at[1])
    to_table.start()
    to_table.wait()
    send_picks(0)
    lax.fori_loop(0, batches // 2, build_pair, 0)
    if batches % 2:
        build(batches - 1, 0)
    for step in range(1, steps + 1):
        if step < steps:
            pass_on(step)
            if step >= 2:
                over(1, group, functools.partial(block_copy, step - 2), wait_send)
            send_picks(step)
        density_step(step - 1)

    load_harms.wait()

    def live_row(batch):
        point = lax.broadcasted_iota(jnp.int32, (1, points), 1)
        return jnp.where(
            point < counts_ref[batch], weights_ref[pl.ds(batch, 1), :], jnp.float32(0.0)
        )

    components = harms.shape[1]
    moment = jnp.zeros((components, points), jnp.float32)
    for batch in range(batches):
        across = slice(batch * points, (batch + 1) * points)
        dens = jnp.sum(rho[:, across], axis=0, keepdims=True)
        rho[0:1, across] = dens
        moment += harms[batch].astype(jnp.float32) * (live_row(batch) * dens)
    diagonal = lax.broadcasted_iota(jnp.int32, (components, LANES), 0) == lax.broadcasted_iota(
        jnp.int32, (components, LANES), 1
    )
    summed = jnp.sum(moment, axis=1, keepdims=True)
    line = jnp.sum(jnp.where(diagonal, summed, 0.0), axis=0, keepdims=True)
    share[...] = jnp.broadcast_to(line, share.shape)
    whose, _ = any_device(0)
    shares[whose] = jnp.broadcast_to(line, share.shape)
    for step in range(steps - 1):
        over(0, row_blocks, functools.partial(ring_copy, step), wait_send)
    for step in range(max(0, steps - 2), steps):
        over(1, group, functools.partial(block_copy, step), wait_send)
    over(1, devices, share_copy, start)
    over(1, devices, share_copy, wait)
    line = jnp.sum(shares[...], axis=0)[0:1]
    total_moment = jnp.sum(jnp.where(diagonal, line, 0.0), axis=1, keepdims=True)
    for batch in range(batches):
        across = slice(batch * points, (batch + 1) * points)
        dens = rho[0:1, across]
        far = FAR_COEFF * jnp.sum(
            total_moment * harms[batch].astype(jnp.float32), axis=0, keepdims=True
        )
        sixth = jnp.exp(jnp.log(1.0 + dens * dens) * (1.0 / 6.0))
        potential = 0.5 * dens - sixth + far / far_scale
        factor[:, across] = jnp.broadcast_to(live_row(batch) * potential, (8, points))

    def scale_rows(step, across):
        ring = lax.rem(ring_me - 1 - step + 2 * steps, steps)
        owner = (ring * inner + across) * row_cap
        spots = [cols_ref[owner + rr] for rr in range(row_cap)]

        def chunk(index, carry):
            span = pl.ds(pl.multiple_of(index * CHUNK, CHUNK), CHUNK)
            for rr in range(row_cap):
                mate = phi[spots[rr], :, span]
                scaled = mate.astype(jnp.float32) * factor[0:1, span]
                rows[rr * BLK : (rr + 1) * BLK, span] = scaled.astype(rows.dtype)
            return carry

        lax.fori_loop(0, all_points // CHUNK, chunk, 0)

    def integral_piece(along, put):
        down = pl.ds(along * col_cap, col_cap)
        term = lax.dot_general(
            rows[...],
            phi[down].reshape(broad, all_points),
            (((1,), (1,)), ((), ())),
            preferred_element_type=jnp.float32,
        )
        for rr in range(row_cap):
            for cr in range(col_cap):
                value = term[rr * BLK : (rr + 1) * BLK, cr * BLK : (cr + 1) * BLK]
                put(rr * col_cap + cr, value.astype(chosen.dtype))

    def send_integrals(step):
        if step >= 2:
            over(1, group, functools.partial(block_copy, step - 2), wait_send)

        def piece(place):
            _, along = target(place)

            def put(index, value):
                chosen[step % 2, place, index] = value

            integral_piece(along, put)

            @pl.when(place < group - 1)
            def _():
                block_copy(step, place + 1).start()

        def far_rows(count, carry):
            shift = inner - 1 - count
            scale_rows(step, lax.rem(inner_me + shift, inner))

            def body(index, inner_carry):
                piece(shift * narrow + narrow - 1 - index)
                return inner_carry

            lax.fori_loop(0, narrow, body, 0)
            return carry

        lax.fori_loop(0, inner - 1, far_rows, 0)
        scale_rows(step, inner_me)

        def near(index, carry):
            piece(narrow - 1 - index)
            return carry

        lax.fori_loop(0, narrow - 1, near, 0)

        def put_own(index, value):
            arrs[step][mine * cap + index] = value

        integral_piece(narrow_me, put_own)
        block_copy(step, 1).start()

    def out_copy(piece):
        return pltpu.make_async_copy(
            ostage.at[piece % 2],
            out_ref.at[pl.ds(pl.multiple_of(piece * BLK, BLK), BLK)],
            out_sem.at[piece % 2],
        )

    def add_up(step):
        last = step == steps - 1
        ring = lax.rem(ring_me - 1 - step + 2 * steps, steps)
        over(1, group, functools.partial(block_copy, step), wait_recv)
        for piece in range(row_blocks):
            if step > 0:
                ring_copy(step - 1, piece).wait_recv()
            if last and piece >= 2:
                out_copy(piece - 2).wait()
            bases = [
                table[one, 2, (ring * inner + inner_me) * row_blocks + piece] + one * cap
                for one in range(group)
            ]

            def add_block(block, carry, piece=piece, bases=bases):
                spot = piece * col_blocks + block
                if step > 0:
                    total = raws[step][spot].astype(jnp.float32)
                else:
                    total = jnp.zeros((BLK, BLK), jnp.float32)
                for one in range(group):
                    col = table[one, 3, narrow_me * col_blocks + block]
                    place = jnp.minimum(bases[one] + col, empty)
                    total += arrs[step][place].astype(jnp.float32)
                if last:
                    across = pl.ds(pl.multiple_of(block * BLK, BLK), BLK)
                    ostage[piece % 2, :, across] = total
                else:
                    raws[step][spot] = total.astype(raws[step].dtype)
                return carry

            lax.fori_loop(0, col_blocks, add_block, 0)
            if last:
                out_copy(piece).start()
            elif piece > 0:
                ring_copy(step, piece - 1).start()
        if not last:
            ring_copy(step, row_blocks - 1).start()
        else:
            for piece in range(max(0, row_blocks - 2), row_blocks):
                out_copy(piece).wait()

    send_integrals(0)
    if steps > 1:
        send_integrals(1)
    for step in range(steps):
        add_up(step)
        if step + 2 < steps:
            send_integrals(step + 2)
    for step in range(max(0, steps - 2), steps):
        over(1, group, functools.partial(block_copy, step), wait_send)
    for step in range(steps - 1):
        over(0, row_blocks, functools.partial(ring_copy, step), wait_send)


def whole_step(inv, cols, counts, tile, weights, dens, orbitals, harmonics, steps, inner, narrow, caps, far_scale):
    row_cap, col_cap = caps
    group = inner * narrow
    cap = row_cap * col_cap
    devices = steps * group
    ring_sems = max(1, steps - 1)
    row_blocks, col_blocks = dens.shape[0] // BLK, dens.shape[1] // BLK
    held = row_blocks * col_blocks
    batches, list_len, _, points = orbitals.shape
    all_points = batches * points
    components = harmonics.shape[1]
    slots = narrow * col_cap
    vmem = pl.BlockSpec(memory_space=pltpu.VMEM)
    smem = pl.BlockSpec(memory_space=pltpu.SMEM)
    anywhere = pl.BlockSpec(memory_space=pl.ANY)
    dma = pltpu.SemaphoreType.DMA
    return pl.pallas_call(
        functools.partial(step_kernel, steps, inner, narrow, row_cap, col_cap, far_scale),
        out_shape=jax.ShapeDtypeStruct(dens.shape, jnp.float32),
        in_specs=[smem] * 3 + [vmem] * 2 + [anywhere] * 3,
        out_specs=anywhere,
        scratch_shapes=[pltpu.VMEM((held, BLK, BLK), dens.dtype)] * steps
        + [pltpu.VMEM((group * cap + 1, BLK, BLK), dens.dtype)] * steps
        + [
            pltpu.VMEM((2, group, cap, BLK, BLK), dens.dtype),
            pltpu.VMEM((group,) + tile.shape, tile.dtype),
            pltpu.SMEM((group,) + tile.shape, tile.dtype),
            pltpu.VMEM((list_len + 1, BLK, points), orbitals.dtype),
            pltpu.VMEM((list_len + 1, BLK, points), orbitals.dtype),
            pltpu.VMEM((slots + 1, BLK, all_points), orbitals.dtype),
            pltpu.VMEM((row_cap * BLK, all_points), orbitals.dtype),
            pltpu.VMEM(harmonics.shape, harmonics.dtype),
            pltpu.VMEM((8, all_points), jnp.float32),
            pltpu.VMEM((8, all_points), jnp.float32),
            pltpu.VMEM((8, LANES), jnp.float32),
            pltpu.VMEM((devices, 8, LANES), jnp.float32),
            pltpu.VMEM((2, BLK, dens.shape[1]), jnp.float32),
            dma((steps, group)),
            dma((steps, group)),
            dma((ring_sems, row_blocks)),
            dma((ring_sems, row_blocks)),
            dma((held,)),
            dma((group,)),
            dma((group,)),
            dma((2,)),
            dma((2,)),
            dma((devices,)),
            dma((devices,)),
            dma((2,)),
        ],
        compiler_params=pltpu.CompilerParams(
            collective_id=1, has_side_effects=True, vmem_limit_bytes=VMEM_BYTES
        ),
        name="grid_step",
    )(inv, cols, counts, tile, weights, dens, orbitals, harmonics)


def rank_among(keys):
    count = keys.shape[0]
    order = jnp.arange(count)
    same = (keys[:, None] == keys[None, :]) & (order[None, :] < order[:, None])
    return jnp.sum(same.astype(jnp.int32), axis=1)


def spread(positions, values, size):
    hit = positions[None, :] == jnp.arange(size)[:, None]
    return jnp.sum(jnp.where(hit, values[None, :], 0), axis=1)


def per_device(
    region, density, block_slot, region_blocks, basis_lists, point_counts, orbitals, weights, harmonics
):
    wide = lax.axis_size("wide")
    narrow = lax.axis_size("narrow")
    devices = wide * narrow
    steps = math.gcd(wide, RING)
    inner = wide // steps
    row_cap = max(1, region // wide)
    col_cap = region // narrow

    known = block_slot.shape[0]
    hit = region_blocks[:, None] == jnp.arange(known)[None, :]
    slots = jnp.sum(jnp.where(hit, block_slot[None, :], 0), axis=1)
    row_owner, row_local = slots % wide, slots // wide
    col_owner, col_local = slots % narrow, slots // narrow
    row_rank, col_rank = rank_among(row_owner), rank_among(col_owner)
    row_place = row_owner * row_cap + row_rank
    col_place = col_owner * col_cap + col_rank
    row_table = spread(row_place, row_local, LANES)
    col_table = spread(col_place, col_local, LANES)
    far = 1 << 20
    row_blocks = density.shape[0] // BLK
    col_blocks = density.shape[1] // BLK
    row_back = far + spread(
        row_owner * row_blocks + row_local, row_rank * col_cap - far, LANES
    )
    col_back = far + spread(col_owner * col_blocks + col_local, col_rank - far, LANES)
    tile = jnp.stack([row_table, col_table, row_back, col_back] * 2)
    none = region
    cols = none + spread(row_place, col_place - none, wide * row_cap)
    list_len = basis_lists.shape[1]
    owner_of = spread(col_place, jnp.arange(region), narrow * col_cap)
    listed = basis_lists[:, :, None] == owner_of[None, None, :]
    order = jnp.arange(list_len)[None, :, None]
    inv = list_len + jnp.sum(jnp.where(listed, order - list_len, 0), axis=1)

    components = harmonics.shape[1]
    batches, _, points = orbitals.shape
    total_points = batches * points * devices
    return whole_step(
        inv,
        cols,
        point_counts,
        tile,
        weights,
        density,
        orbitals.reshape(batches, list_len, BLK, points),
        harmonics,
        steps,
        inner,
        narrow,
        (row_cap, col_cap),
        math.sqrt(total_points * components),
    )


def solution(mesh):
    devices = mesh.shape["wide"] * mesh.shape["narrow"]

    def whole(density, block_slot, region_blocks, *others):
        region = region_blocks.shape[0] // devices
        in_specs = (
            P("wide", "narrow"),
            P(),
            P(("wide", "narrow")),
            P(("wide", "narrow"), None),
            P(("wide", "narrow")),
            P(("wide", "narrow"), None, None),
            P(("wide", "narrow"), None),
            P(("wide", "narrow"), None, None),
        )
        mapped = jax.shard_map(
            functools.partial(per_device, region),
            mesh=mesh,
            in_specs=in_specs,
            out_specs=P("wide", "narrow"),
            check_vma=False,
        )
        return mapped(density, block_slot, region_blocks, *others)

    return whole
```

time: 248 us -> 227 us (0.915); the launches traced: 245 us -> 226 us
  Pallas kernels: 237 us -> 219 us
    pallas_call x3 -> x1, Pallas kernels: 237 us -> 219 us  [whole_step(): pl.pallas_call(functools.partial(step_kernel, steps, inner, narrow, row_c...]
where the time goes in v1:
time: 227 us; the launch traced here: 226 us
  Pallas kernels  219 us (96%)
  local copies, waits for them, and re-layouts  4.54 us (2%)
  other arithmetic  2.81 us (1%)
    pallas_call x1, Pallas kernels, whole_step(): pl.pallas_call(functools.partial(step_kernel, steps, inner, narrow, row_c...  219 us

profile of v1, /device:TPU:0, one launch (start us, length us, event | category | flops | bytes accessed | tf_op | source)
XLA Modules:
  0.0 226.5 jit_solution(12393401517722709107)
XLA Ops:
  0.0 0.9 select_reduce_fusion.7
  0.9 0.2 convert_reduce_fusion
  1.1 0.2 convert_reduce_fusion.1
  1.3 0.1 select_reduce_fusion.1
  1.4 0.1 select_reduce_fusion.3
  1.5 0.1 select_reduce_fusion.5
  1.6 0.6 broadcast_add_fusion.2.cols_ref
  2.1 0.6 stack.8.tile_ref
  2.7 0.8 copy.10
  3.5 0.1 select_reduce_fusion
  3.6 0.6 broadcast_add_fusion.inv_ref
  4.2 219.1 %grid_step.1 = f32[512,1024]{1,0:T(8,128)} custom-call(s32[12,16]{1,0:T(8,128)} %broadcast_add_fusion.inv_ref, s32[16]{0:T(128)} %broadcast_add_fusion.2.cols_ref, s32[12]{0:T(128)} %counts_ref.1, s32[8,128]{1,0:T(8,128)} %stack.8.tile_ref, f32[12,256]{1,0:T(8,128)} %weights_ref.1, bf16[512,1024]{1,0:T(8,128)(2,1)} %dens_ref.1, ...), custom_call_target="tpu_custom_call" | custom-call | tf_op jit(solution)/shard_map/grid_step/pallas_call | solution.py:509
  223.3 3.2 %copy.12 = f32[512,1024]{1,0:T(8,128)} copy(f32[512,1024]{1,0:T(8,128)} %grid_step.1) | data formatting | bytes 4194304
  (6 shorter events, 0.0 us)

commit v2 on v1

v2 whole, which is shorter than its diff:
```python
import functools
import math

import jax
import jax.numpy as jnp
from jax import lax
from jax.experimental import pallas as pl
from jax.experimental.pallas import tpu as pltpu
from jax.sharding import PartitionSpec as P

BLK = 128
FAR_COEFF = 10.0
RING = 4
LANES = 128
CHUNK = 512
HALVES = 2
HALF = BLK // HALVES
MESH = pl.DeviceIdType.MESH
VMEM_BYTES = 63 * 1024 * 1024


def ring_device(shift, inner):
    wide = lax.axis_size("wide")
    return (lax.rem(lax.axis_index("wide") + shift * inner + wide, wide), lax.axis_index("narrow"))


def any_device(offset):
    narrow = lax.axis_size("narrow")
    devices = lax.axis_size("wide") * narrow
    mine = lax.axis_index("wide") * narrow + lax.axis_index("narrow")
    other = lax.rem(mine + offset, devices)
    return mine, (other // narrow, other % narrow)


def step_kernel(
    steps,
    inner,
    narrow,
    row_cap,
    col_cap,
    far_scale,
    slot_ref,
    region_ref,
    lists_ref,
    counts_ref,
    weights_ref,
    dens_ref,
    orb_ref,
    harm_ref,
    out_ref,
    *rest,
):
    count = steps * HALVES
    raws = [rest[step * HALVES : (step + 1) * HALVES] for step in range(steps)]
    arrs = [rest[count + step * HALVES : count + (step + 1) * HALVES] for step in range(steps)]
    rest = rest[2 * count :]
    (
        chosen,
        slot_of,
        region_of,
        lists,
        counts,
        weights,
        places,
        tile,
        own_inv,
        inv,
        tables,
        table,
        even,
        odd,
        phi,
        rows,
        harms,
        rho,
        factor,
        share,
        shares,
        ostage,
        send_sem,
        recv_sem,
        ring_send,
        ring_recv,
        load_sem,
        tile_send,
        tile_recv,
        orb_sem,
        local_sem,
        int_sem,
        share_send,
        share_recv,
        out_sem,
    ) = rest
    devices = lax.axis_size("wide") * narrow
    group = inner * narrow
    cap = row_cap * col_cap
    wide_me = lax.axis_index("wide")
    inner_me = wide_me % inner
    ring_me = wide_me // inner
    base = ring_me * inner
    narrow_me = lax.axis_index("narrow")
    mine = inner_me * narrow + narrow_me
    col_blocks = dens_ref.shape[1] // BLK
    row_blocks = dens_ref.shape[0] // BLK
    held = row_blocks * col_blocks
    empty = group * cap
    batches, list_len, _, points = orb_ref.shape
    all_points = batches * points
    slots = narrow * col_cap
    tall = row_cap * BLK
    broad = col_cap * BLK

    def target(place):
        across = lax.rem(inner_me + place // narrow, inner)
        along = lax.rem(narrow_me + place % narrow, narrow)
        return across, along

    def source(place):
        across = lax.rem(inner_me + inner - place // narrow, inner)
        along = lax.rem(narrow_me + narrow - place % narrow, narrow)
        return across, along

    def load_copy(half, place):
        row, col = place // col_blocks, place % col_blocks
        return pltpu.make_async_copy(
            dens_ref.at[
                pl.ds(pl.multiple_of(row * BLK + half * HALF, HALF), HALF),
                pl.ds(pl.multiple_of(col * BLK, BLK), BLK),
            ],
            raws[0][half].at[place],
            load_sem.at[half],
        )

    def loaded(half):
        pltpu.make_async_copy(raws[0][half], raws[0][half], load_sem.at[half]).wait()

    stages = (even, odd)

    def orb_copy(batch, which):
        return pltpu.make_async_copy(
            orb_ref.at[batch], stages[which].at[pl.ds(0, list_len)], orb_sem.at[which]
        )

    def block_copy(step, half, place):
        across, along = target(place)
        return pltpu.make_async_remote_copy(
            src_ref=chosen.at[step % 2, half, place],
            dst_ref=arrs[step][half].at[pl.ds(mine * cap, cap)],
            send_sem=send_sem.at[step, half, place],
            recv_sem=recv_sem.at[step, half, place],
            device_id=(base + across, along),
            device_id_type=MESH,
        )

    def ring_copy(step, half, piece):
        span = pl.ds(piece * col_blocks, col_blocks)
        return pltpu.make_async_remote_copy(
            src_ref=raws[step][half].at[span],
            dst_ref=raws[step + 1][half].at[span],
            send_sem=ring_send.at[step, half, piece],
            recv_sem=ring_recv.at[step, half, piece],
            device_id=ring_device(1, inner),
            device_id_type=MESH,
        )

    def tile_copy(place):
        across, along = target(place)
        return pltpu.make_async_remote_copy(
            src_ref=tile,
            dst_ref=tables.at[mine],
            send_sem=tile_send.at[place],
            recv_sem=tile_recv.at[place],
            device_id=(base + across, along),
            device_id_type=MESH,
        )

    def share_copy(offset):
        whose, device = any_device(offset)
        return pltpu.make_async_remote_copy(
            src_ref=share,
            dst_ref=shares.at[whose],
            send_sem=share_send.at[offset],
            recv_sem=share_recv.at[offset],
            device_id=device,
            device_id_type=MESH,
        )

    def over(first, last, make, act):
        def body(index, carry):
            act(make(index))
            return carry

        lax.fori_loop(first, last, body, 0)

    start = lambda copy: copy.start()
    wait = lambda copy: copy.wait()
    wait_send = lambda copy: copy.wait_send()
    wait_recv = lambda copy: copy.wait_recv()

    barrier = pltpu.get_barrier_semaphore()

    def greet(place, carry):
        across, along = target(place)
        pl.semaphore_signal(barrier, inc=1, device_id=(base + across, along), device_id_type=MESH)
        return carry

    lax.fori_loop(1, group, greet, 0)
    if steps > 1:
        for shift in (1, -1):
            pl.semaphore_signal(
                barrier, inc=1, device_id=ring_device(shift, inner), device_id_type=MESH
            )
    integers = [
        pltpu.make_async_copy(given, held_in, int_sem.at[index])
        for index, (given, held_in) in enumerate(
            ((slot_ref, slot_of), (region_ref, region_of), (lists_ref, lists), (counts_ref, counts))
        )
    ]
    for copy in integers:
        copy.start()
    for half in range(HALVES):
        over(0, held, functools.partial(load_copy, half), start)
    for which in range(min(2, batches)):
        orb_copy(which, which).start()
    load_harms = pltpu.make_async_copy(harm_ref, harms, local_sem.at[0])
    load_harms.start()
    load_weights = pltpu.make_async_copy(weights_ref, weights, local_sem.at[2])
    load_weights.start()
    for step in range(steps):
        for half in range(HALVES):
            arrs[step][half][empty] = jnp.zeros((HALF, BLK), chosen.dtype)
    for stage in stages:
        stage[list_len] = jnp.zeros((BLK, points), stage.dtype)
    phi[slots] = jnp.zeros((BLK, all_points), phi.dtype)
    rho[...] = jnp.zeros_like(rho)
    for copy in integers:
        copy.wait()

    region = region_of.shape[0]
    wide = lax.axis_size("wide")
    named = [slot_of[region_of[spot]] for spot in range(region)]
    lane = lax.broadcasted_iota(jnp.int32, (8, LANES), 1)
    line = lax.broadcasted_iota(jnp.int32, (8, LANES), 0)
    far = 1 << 20
    row_table = jnp.zeros((8, LANES), jnp.int32)
    col_table = jnp.zeros((8, LANES), jnp.int32)
    row_back = jnp.full((8, LANES), far, jnp.int32)
    col_back = jnp.full((8, LANES), far, jnp.int32)
    cross = jnp.full((8, LANES), slots, jnp.int32)
    row_owners = [lax.rem(slot, wide) for slot in named]
    col_owners = [lax.rem(slot, narrow) for slot in named]
    for spot in range(region):
        row_local, col_local = named[spot] // wide, named[spot] // narrow
        row_rank, col_rank = jnp.int32(0), jnp.int32(0)
        for earlier in range(spot):
            row_rank += (row_owners[earlier] == row_owners[spot]).astype(jnp.int32)
            col_rank += (col_owners[earlier] == col_owners[spot]).astype(jnp.int32)
        row_place = row_owners[spot] * row_cap + row_rank
        col_place = col_owners[spot] * col_cap + col_rank
        places[spot] = col_place
        row_table = jnp.where(lane == row_place, row_local, row_table)
        col_table = jnp.where(lane == col_place, col_local, col_table)
        row_back = jnp.where(
            lane == row_owners[spot] * row_blocks + row_local, row_rank * col_cap, row_back
        )
        col_back = jnp.where(lane == col_owners[spot] * col_blocks + col_local, col_rank, col_back)
        cross = jnp.where(lane == row_place, col_place, cross)
    index_tile = jnp.where(line == 0, row_table, cross)
    index_tile = jnp.where(line == 1, col_table, index_tile)
    index_tile = jnp.where(line == 2, row_back, index_tile)
    index_tile = jnp.where(line == 3, col_back, index_tile)
    tile[...] = index_tile
    tables[mine] = index_tile
    pl.semaphore_wait(barrier, group - 1 + (2 if steps > 1 else 0))
    over(1, group, tile_copy, start)

    def pass_on(step, half):
        for piece in range(row_blocks):
            if step > 0:
                ring_copy(step - 1, half, piece).wait_recv()
            if step < steps - 1:
                ring_copy(step, half, piece).start()

    def pick(step, half, place, put):
        across, along = target(place)
        other = across * narrow + along
        ring = lax.rem(ring_me - step + steps, steps)
        for rr in range(row_cap):
            row = table[other, 0, (ring * inner + inner_me) * row_cap + rr] * col_blocks
            for cr in range(col_cap):
                spot = row + table[other, 1, narrow_me * col_cap + cr]
                put(rr * col_cap + cr, raws[step][half][spot])

    def send_picks(step, half):
        if step >= 2:
            over(1, group, functools.partial(block_copy, step - 2, half), wait_send)

        def put_own(index, value):
            arrs[step][half][mine * cap + index] = value

        def body(count, carry):
            place = group - 1 - count

            def put(index, value):
                chosen[step % 2, half, place, index] = value

            pick(step, half, place, put)

            @pl.when(count > 0)
            def _():
                block_copy(step, half, place + 1).start()

            return carry

        lax.fori_loop(0, group - 1, body, 0)
        pick(step, half, 0, put_own)
        block_copy(step, half, 1).start()

    def density_piece(step, halves, place):
        across, along = source(place)
        first = (across * narrow + along) * cap
        ring = lax.rem(ring_me - step + steps, steps)
        owner = (ring * inner + across) * row_cap
        block = jnp.concatenate(
            [
                jnp.concatenate(
                    [arrs[step][half][first + rr * col_cap + cr] for cr in range(col_cap)], axis=1
                )
                for rr in range(row_cap)
                for half in halves
            ],
            axis=0,
        )
        spots = [table[mine, 4, owner + rr] for rr in range(row_cap)]
        down = pl.ds(along * col_cap, col_cap)
        low, size = halves[0] * HALF, len(halves) * HALF

        def chunk(index, carry):
            span = pl.ds(pl.multiple_of(index * CHUNK, CHUNK), CHUNK)
            wave = phi[down, :, span].reshape(broad, CHUNK)
            product = jnp.dot(block, wave, preferred_element_type=jnp.float32)
            total = rho[:, span]
            for rr in range(row_cap):
                mate = phi[spots[rr], low : low + size, span]
                part = product[rr * size : (rr + 1) * size] * mate.astype(jnp.float32)
                total += jnp.sum(part.reshape(size // 8, 8, CHUNK), axis=0)
            rho[:, span] = total
            return carry

        lax.fori_loop(0, all_points // CHUNK, chunk, 0, unroll=True)

    def density_pieces(step, halves, first, last):
        def body(count, carry):
            place = group - 1 - count
            for half in halves:
                block_copy(step, half, place).wait_recv()
            density_piece(step, halves, place)
            return carry

        lax.fori_loop(first, last, body, 0)

    def build(batch, which):
        orb_copy(batch, which).wait()
        across = pl.ds(pl.multiple_of(batch * points, points), points)
        for slot in range(slots):
            phi[slot, :, across] = stages[which][inv[batch, slot]]

        @pl.when(batch + 2 < batches)
        def _():
            orb_copy(batch + 2, which).start()

    def build_pair(pair, carry):
        for which in range(2):
            build(pair * 2 + which, which)
        return carry

    both = tuple(range(HALVES))
    for half in both:
        loaded(half)
        pass_on(0, half)
    over(1, group, tile_copy, wait)
    to_table = pltpu.make_async_copy(tables, table, local_sem.at[1])
    to_table.start()
    to_table.wait()
    for half in both:
        send_picks(0, half)
    for batch in range(batches):
        found = jnp.full((8, LANES), list_len, jnp.int32)
        for spot in range(list_len):
            found = jnp.where(lane == places[lists[batch, spot]], spot, found)
        own_inv[batch : batch + 1, :] = found[0:1]
    to_inv = pltpu.make_async_copy(own_inv, inv, local_sem.at[3])
    to_inv.start()
    to_inv.wait()
    lax.fori_loop(0, batches // 2, build_pair, 0)
    if batches % 2:
        build(batches - 1, 0)
    middle = group // 2
    for step in range(1, steps):
        pass_on(step, 0)
        send_picks(step, 0)
        density_pieces(step - 1, both, 0, middle)
        pass_on(step, 1)
        send_picks(step, 1)
        density_pieces(step - 1, both, middle, group - 1)
        density_piece(step - 1, both, 0)
    for half in both:
        density_piece(steps - 1, (half,), 0)
        density_pieces(steps - 1, (half,), 0, group - 1)

    load_harms.wait()
    load_weights.wait()

    def live_row(batch):
        point = lax.broadcasted_iota(jnp.int32, (1, points), 1)
        return jnp.where(
            point < counts[batch], weights[pl.ds(batch, 1), :], jnp.float32(0.0)
        )

    components = harms.shape[1]
    moment = jnp.zeros((components, points), jnp.float32)
    for batch in range(batches):
        across = slice(batch * points, (batch + 1) * points)
        dens = jnp.sum(rho[:, across], axis=0, keepdims=True)
        rho[0:1, across] = dens
        moment += harms[batch].astype(jnp.float32) * (live_row(batch) * dens)
    diagonal = lax.broadcasted_iota(jnp.int32, (components, LANES), 0) == lax.broadcasted_iota(
        jnp.int32, (components, LANES), 1
    )
    summed = jnp.sum(moment, axis=1, keepdims=True)
    line = jnp.sum(jnp.where(diagonal, summed, 0.0), axis=0, keepdims=True)
    share[...] = jnp.broadcast_to(line, share.shape)
    whose, _ = any_device(0)
    shares[whose] = jnp.broadcast_to(line, share.shape)
    for half in both:
        for step in range(steps - 1):
            over(0, row_blocks, functools.partial(ring_copy, step, half), wait_send)
        for step in range(max(0, steps - 2), steps):
            over(1, group, functools.partial(block_copy, step, half), wait_send)
    over(1, devices, share_copy, start)
    over(1, devices, share_copy, wait)
    line = jnp.sum(shares[...], axis=0)[0:1]
    total_moment = jnp.sum(jnp.where(diagonal, line, 0.0), axis=1, keepdims=True)
    for batch in range(batches):
        across = slice(batch * points, (batch + 1) * points)
        dens = rho[0:1, across]
        far = FAR_COEFF * jnp.sum(
            total_moment * harms[batch].astype(jnp.float32), axis=0, keepdims=True
        )
        sixth = jnp.exp(jnp.log(1.0 + dens * dens) * (1.0 / 6.0))
        potential = 0.5 * dens - sixth + far / far_scale
        factor[:, across] = jnp.broadcast_to(live_row(batch) * potential, (8, points))

    def scale_rows(step, across):
        ring = lax.rem(ring_me - 1 - step + 2 * steps, steps)
        owner = (ring * inner + across) * row_cap
        spots = [table[mine, 4, owner + rr] for rr in range(row_cap)]

        def chunk(index, carry):
            span = pl.ds(pl.multiple_of(index * CHUNK, CHUNK), CHUNK)
            for rr in range(row_cap):
                mate = phi[spots[rr], :, span]
                scaled = mate.astype(jnp.float32) * factor[0:1, span]
                rows[rr * BLK : (rr + 1) * BLK, span] = scaled.astype(rows.dtype)
            return carry

        lax.fori_loop(0, all_points // CHUNK, chunk, 0)

    def integral_piece(along, put):
        down = pl.ds(along * col_cap, col_cap)
        term = lax.dot_general(
            rows[...],
            phi[down].reshape(broad, all_points),
            (((1,), (1,)), ((), ())),
            preferred_element_type=jnp.float32,
        )
        for rr in range(row_cap):
            for cr in range(col_cap):
                value = term[rr * BLK : (rr + 1) * BLK, cr * BLK : (cr + 1) * BLK]
                put(rr * col_cap + cr, value.astype(chosen.dtype))

    def send_integrals(step):
        if step >= 2:
            for half in both:
                over(1, group, functools.partial(block_copy, step - 2, half), wait_send)

        def piece(place):
            _, along = target(place)

            def put(index, value):
                for half in both:
                    chosen[step % 2, half, place, index] = value[half * HALF : (half + 1) * HALF]

            integral_piece(along, put)

            @pl.when(place < group - 1)
            def _():
                block_copy(step, 0, place + 1).start()

        def far_rows(count, carry):
            shift = inner - 1 - count
            scale_rows(step, lax.rem(inner_me + shift, inner))

            def body(index, inner_carry):
                piece(shift * narrow + narrow - 1 - index)
                return inner_carry

            lax.fori_loop(0, narrow, body, 0)
            return carry

        lax.fori_loop(0, inner - 1, far_rows, 0)
        scale_rows(step, inner_me)

        def near(index, carry):
            piece(narrow - 1 - index)
            return carry

        lax.fori_loop(0, narrow - 1, near, 0)

        def put_own(index, value):
            for half in both:
                arrs[step][half][mine * cap + index] = value[half * HALF : (half + 1) * HALF]

        integral_piece(narrow_me, put_own)
        block_copy(step, 0, 1).start()

        def later(count, carry):
            block_copy(step, 1, group - 1 - count).start()
            return carry

        lax.fori_loop(0, group - 1, later, 0)

    def out_copy(half, piece):
        first = pl.multiple_of(piece * BLK + half * HALF, HALF)
        return pltpu.make_async_copy(
            ostage.at[piece % 2], out_ref.at[pl.ds(first, HALF)], out_sem.at[piece % 2]
        )

    def add_up(step, half):
        last = step == steps - 1
        ring = lax.rem(ring_me - 1 - step + 2 * steps, steps)
        over(1, group, functools.partial(block_copy, step, half), wait_recv)
        for piece in range(row_blocks):
            if step > 0:
                ring_copy(step - 1, half, piece).wait_recv()
            if last and piece >= 2:
                out_copy(half, piece - 2).wait()
            bases = [
                table[one, 2, (ring * inner + inner_me) * row_blocks + piece] + one * cap
                for one in range(group)
            ]

            def add_block(block, carry, piece=piece, bases=bases):
                spot = piece * col_blocks + block
                if step > 0:
                    total = raws[step][half][spot].astype(jnp.float32)
                else:
                    total = jnp.zeros((HALF, BLK), jnp.float32)
                for one in range(group):
                    col = table[one, 3, narrow_me * col_blocks + block]
                    place = jnp.minimum(bases[one] + col, empty)
                    total += arrs[step][half][place].astype(jnp.float32)
                if last:
                    across = pl.ds(pl.multiple_of(block * BLK, BLK), BLK)
                    ostage[piece % 2, :, across] = total
                else:
                    raws[step][half][spot] = total.astype(chosen.dtype)
                return carry

            lax.fori_loop(0, col_blocks, add_block, 0)
            if last:
                out_copy(half, piece).start()
            elif piece > 0:
                ring_copy(step, half, piece - 1).start()
        if not last:
            ring_copy(step, half, row_blocks - 1).start()
        else:
            for piece in range(max(0, row_blocks - 2), row_blocks):
                out_copy(half, piece).wait()

    send_integrals(0)
    for step in range(steps):
        add_up(step, 0)
        if step + 1 < steps:
            send_integrals(step + 1)
        add_up(step, 1)
    for half in both:
        for step in range(max(0, steps - 2), steps):
            over(1, group, functools.partial(block_copy, step, half), wait_send)
        for step in range(steps - 1):
            over(0, row_blocks, functools.partial(ring_copy, step, half), wait_send)


def whole_step(
    block_slot, region_blocks, lists, counts, weights, dens, orbitals, harmonics, steps, inner, narrow, caps, far_scale
):
    row_cap, col_cap = caps
    group = inner * narrow
    cap = row_cap * col_cap
    devices = steps * group
    ring_sems = max(1, steps - 1)
    row_blocks, col_blocks = dens.shape[0] // BLK, dens.shape[1] // BLK
    held = row_blocks * col_blocks
    batches, list_len, _, points = orbitals.shape
    all_points = batches * points
    components = harmonics.shape[1]
    slots = narrow * col_cap
    ints = jnp.int32
    anywhere = pl.BlockSpec(memory_space=pl.ANY)
    dma = pltpu.SemaphoreType.DMA
    return pl.pallas_call(
        functools.partial(step_kernel, steps, inner, narrow, row_cap, col_cap, far_scale),
        out_shape=jax.ShapeDtypeStruct(dens.shape, jnp.float32),
        in_specs=[anywhere] * 8,
        out_specs=anywhere,
        scratch_shapes=[pltpu.VMEM((held, HALF, BLK), dens.dtype)] * (steps * HALVES)
        + [pltpu.VMEM((group * cap + 1, HALF, BLK), dens.dtype)] * (steps * HALVES)
        + [
            pltpu.VMEM((2, HALVES, group, cap, HALF, BLK), dens.dtype),
            pltpu.SMEM(block_slot.shape, ints),
            pltpu.SMEM(region_blocks.shape, ints),
            pltpu.SMEM(lists.shape, ints),
            pltpu.SMEM(counts.shape, ints),
            pltpu.VMEM(weights.shape, weights.dtype),
            pltpu.SMEM(region_blocks.shape, ints),
            pltpu.VMEM((8, LANES), ints),
            pltpu.VMEM((-(-batches // 8) * 8, LANES), ints),
            pltpu.SMEM((-(-batches // 8) * 8, LANES), ints),
            pltpu.VMEM((group, 8, LANES), ints),
            pltpu.SMEM((group, 8, LANES), ints),
            pltpu.VMEM((list_len + 1, BLK, points), orbitals.dtype),
            pltpu.VMEM((list_len + 1, BLK, points), orbitals.dtype),
            pltpu.VMEM((slots + 1, BLK, all_points), orbitals.dtype),
            pltpu.VMEM((row_cap * BLK, all_points), orbitals.dtype),
            pltpu.VMEM(harmonics.shape, harmonics.dtype),
            pltpu.VMEM((8, all_points), jnp.float32),
            pltpu.VMEM((8, all_points), jnp.float32),
            pltpu.VMEM((8, LANES), jnp.float32),
            pltpu.VMEM((devices, 8, LANES), jnp.float32),
            pltpu.VMEM((2, HALF, dens.shape[1]), jnp.float32),
            dma((steps, HALVES, group)),
            dma((steps, HALVES, group)),
            dma((ring_sems, HALVES, row_blocks)),
            dma((ring_sems, HALVES, row_blocks)),
            dma((HALVES,)),
            dma((group,)),
            dma((group,)),
            dma((2,)),
            dma((4,)),
            dma((4,)),
            dma((devices,)),
            dma((devices,)),
            dma((2,)),
        ],
        compiler_params=pltpu.CompilerParams(
            collective_id=1, has_side_effects=True, vmem_limit_bytes=VMEM_BYTES
        ),
        name="grid_step",
    )(block_slot, region_blocks, lists, counts, weights, dens, orbitals, harmonics)


def per_device(
    region, density, block_slot, region_blocks, basis_lists, point_counts, orbitals, weights, harmonics
):
    wide = lax.axis_size("wide")
    narrow = lax.axis_size("narrow")
    devices = wide * narrow
    steps = math.gcd(wide, RING)
    inner = wide // steps
    row_cap = max(1, region // wide)
    col_cap = region // narrow

    components = harmonics.shape[1]
    batches, _, points = orbitals.shape
    total_points = batches * points * devices
    return whole_step(
        block_slot,
        region_blocks,
        basis_lists,
        point_counts,
        weights,
        density,
        orbitals.reshape(batches, -1, BLK, points),
        harmonics,
        steps,
        inner,
        narrow,
        (row_cap, col_cap),
        math.sqrt(total_points * components),
    )


def solution(mesh):
    devices = mesh.shape["wide"] * mesh.shape["narrow"]

    def whole(density, block_slot, region_blocks, *others):
        region = region_blocks.shape[0] // devices
        in_specs = (
            P("wide", "narrow"),
            P(),
            P(("wide", "narrow")),
            P(("wide", "narrow"), None),
            P(("wide", "narrow")),
            P(("wide", "narrow"), None, None),
            P(("wide", "narrow"), None),
            P(("wide", "narrow"), None, None),
        )
        mapped = jax.shard_map(
            functools.partial(per_device, region),
            mesh=mesh,
            in_specs=in_specs,
            out_specs=P("wide", "narrow"),
            check_vma=False,
        )
        return mapped(density, block_slot, region_blocks, *others)

    return whole
```

time: 227 us -> 216 us (0.952)
  Pallas kernels: 219 us -> 211 us
  other arithmetic: 2.81 us -> 0 us
    pallas_call x1, Pallas kernels: 219 us -> 211 us  [whole_step(): pl.pallas_call(functools.partial(step_kernel, steps, inner, narrow, row_c...]
where the time goes in v2:
time: 216 us
  Pallas kernels  211 us (98%)
  local copies, waits for them, and re-layouts  4.52 us (2%)
    pallas_call x1, Pallas kernels, whole_step(): pl.pallas_call(functools.partial(step_kernel, steps, inner, narrow, row_c...  211 us
    unnamed x2, local copies, waits for them, and re-layouts  4.52 us

profile of v2, /device:TPU:0, one launch (start us, length us, event | category | flops | bytes accessed | tf_op | source)
XLA Modules:
  0.0 215.7 jit_solution(16226576780401300372)
XLA Ops:
  0.0 1.4 copy.9.lists_ref
  1.4 211.2 %grid_step.1 = f32[512,1024]{1,0:T(8,128)} custom-call(s32[32]{0:T(128)} %slot_ref.1, s32[16]{0:T(128)} %region_ref.1, s32[12,8]{1,0:T(8,128)} %copy.9.lists_ref, s32[12]{0:T(128)} %counts_ref.1, f32[12,256]{1,0:T(8,128)} %weights_ref.1, bf16[512,1024]{1,0:T(8,128)(2,1)} %dens_ref.1, bf16[12,8,128,256]{3,2,1,0:T(8,128)(2,1)} %bitcast.1, ...), custom_call_target="tpu_custom_call" | custom-call | tf_op jit(solution)/shard_map/grid_step/pallas_call | solution.py:611
  212.6 3.2 %copy.11 = f32[512,1024]{1,0:T(8,128)} copy(f32[512,1024]{1,0:T(8,128)} %grid_step.1) | data formatting | bytes 4194304

commit v3 on v2

--- a/solution.py
+++ b/solution.py
@@ -30,6 +30,10 @@
     mine = lax.axis_index("wide") * narrow + lax.axis_index("narrow")
     other = lax.rem(mine + offset, devices)
     return mine, (other // narrow, other % narrow)
+
+
+def trades(inner, narrow):
+    return inner == 2 and narrow == 4 and HALVES == 2
 
 
 def step_kernel(
@@ -54,6 +58,10 @@
     raws = [rest[step * HALVES : (step + 1) * HALVES] for step in range(steps)]
     arrs = [rest[count + step * HALVES : count + (step + 1) * HALVES] for step in range(steps)]
     rest = rest[2 * count :]
+    square = trades(inner, narrow)
+    if square:
+        swaps, swap_send, swap_recv = rest[:HALVES], rest[HALVES], rest[HALVES + 1]
+        rest = rest[HALVES + 2 :]
     (
         chosen,
         slot_of,
@@ -163,6 +171,38 @@
             device_id_type=MESH,
         )
 
+    def swap_place(half):
+        if half == 0:
+            return 1 - inner_me, narrow_me
+        return inner_me, lax.rem(narrow_me + narrow // 2, narrow)
+
+    def swap_copy(half):
+        across, along = swap_place(half)
+        return pltpu.make_async_remote_copy(
+            src_ref=raws[0][half],
+            dst_ref=swaps[half],
+            send_sem=swap_send.at[half],
+            recv_sem=swap_recv.at[half],
+            device_id=(base + across, along),
+            device_id_type=MESH,
+        )
+
+    def over_blocks(step, half, act, first=1, last=group, plain=False):
+        local = (narrow, narrow // 2)[half] if square and step == 0 and not plain else 0
+
+        def body(place, carry):
+            if local:
+
+                @pl.when(place != local)
+                def _():
+                    act(block_copy(step, half, place))
+
+            else:
+                act(block_copy(step, half, place))
+            return carry
+
+        lax.fori_loop(first, last, body, 0)
+
     def tile_copy(place):
         across, along = target(place)
         return pltpu.make_async_remote_copy(
@@ -293,7 +333,7 @@
 
     def send_picks(step, half):
         if step >= 2:
-            over(1, group, functools.partial(block_copy, step - 2, half), wait_send)
+            over_blocks(step - 2, half, wait_send)
 
         def put_own(index, value):
             arrs[step][half][mine * cap + index] = value
@@ -315,6 +355,53 @@
         lax.fori_loop(0, group - 1, body, 0)
         pick(step, half, 0, put_own)
         block_copy(step, half, 1).start()
+
+    def trade(half, ours):
+        other_side = swap_place(half)
+        across_s, along_s = (inner_me, narrow_me) if ours else other_side
+        held_in = raws[0][half] if ours else swaps[half]
+        slot = (across_s * narrow + along_s) * cap
+
+        def choose(across, along, put):
+            one = across * narrow + along
+            for rr in range(row_cap):
+                row = table[one, 0, (base + across_s) * row_cap + rr] * col_blocks
+                for cr in range(col_cap):
+                    spot = row + table[one, 1, along_s * col_cap + cr]
+                    put(rr * col_cap + cr, held_in[spot])
+
+        def put_own(index, value):
+            arrs[0][half][slot + index] = value
+
+        copies = []
+        for turn in (1, 2, 3):
+            if half == 0:
+                across, along = inner_me, lax.rem(narrow_me + turn, narrow)
+            else:
+                across = lax.rem(inner_me + turn // 2, inner)
+                along = narrow_me // 2 * 2 + lax.rem(narrow_me + turn, 2)
+            place = lax.rem(across + inner - across_s, inner) * narrow + lax.rem(
+                along + narrow - along_s, narrow
+            )
+
+            def put(index, value, place=place):
+                chosen[0, half, place, index] = value
+
+            choose(across, along, put)
+            copies.append(
+                pltpu.make_async_remote_copy(
+                    src_ref=chosen.at[0, half, place],
+                    dst_ref=arrs[0][half].at[pl.ds(slot, cap)],
+                    send_sem=send_sem.at[0, half, place],
+                    recv_sem=recv_sem.at[0, half, place],
+                    device_id=(base + across, along),
+                    device_id_type=MESH,
+                )
+            )
+            if len(copies) > 1:
+                copies[-2].start()
+        choose(inner_me, narrow_me, put_own)
+        copies[-1].start()
 
     def density_piece(step, halves, place):
         across, along = source(place)
@@ -353,7 +440,7 @@
         def body(count, carry):
             place = group - 1 - count
             for half in halves:
-                block_copy(step, half, place).wait_recv()
+                over_blocks(step, half, wait_recv, place, place + 1)
             density_piece(step, halves, place)
             return carry
 
@@ -377,17 +464,22 @@
     both = tuple(range(HALVES))
     for half in both:
         loaded(half)
+        if square:
+            swap_copy(half).start()
         pass_on(0, half)
     over(1, group, tile_copy, wait)
     to_table = pltpu.make_async_copy(tables, table, local_sem.at[1])
     to_table.start()
     to_table.wait()
     for half in both:
-        send_picks(0, half)
+        if square:
+            trade(half, True)
+        else:
+            send_picks(0, half)
     for batch in range(batches):
         found = jnp.full((8, LANES), list_len, jnp.int32)
         for spot in range(list_len):
-            found = jnp.where(lane == places[lists[batch, spot]], spot, found)
+            found = jnp.where(lane == places[lists[spot, batch]], spot, found)
         own_inv[batch : batch + 1, :] = found[0:1]
     to_inv = pltpu.make_async_copy(own_inv, inv, local_sem.at[3])
     to_inv.start()
@@ -395,8 +487,12 @@
     lax.fori_loop(0, batches // 2, build_pair, 0)
     if batches % 2:
         build(batches - 1, 0)
-    middle = group // 2
+    if square:
+        for half in both:
+            swap_copy(half).wait_recv()
+            trade(half, False)
     for step in range(1, steps):
+        middle = group // 2 if step > 1 else 0
         pass_on(step, 0)
         send_picks(step, 0)
         density_pieces(step - 1, both, 0, middle)
@@ -436,7 +532,10 @@
         for step in range(steps - 1):
             over(0, row_blocks, functools.partial(ring_copy, step, half), wait_send)
         for step in range(max(0, steps - 2), steps):
-            over(1, group, functools.partial(block_copy, step, half), wait_send)
+            over_blocks(step, half, wait_send)
+    if square:
+        for half in both:
+            swap_copy(half).wait_send()
     over(1, devices, share_copy, start)
     over(1, devices, share_copy, wait)
     line = jnp.sum(shares[...], axis=0)[0:1]
@@ -482,7 +581,7 @@
     def send_integrals(step):
         if step >= 2:
             for half in both:
-                over(1, group, functools.partial(block_copy, step - 2, half), wait_send)
+                over_blocks(step - 2, half, wait_send, plain=True)
 
         def piece(place):
             _, along = target(place)
@@ -608,6 +707,10 @@
     ints = jnp.int32
     anywhere = pl.BlockSpec(memory_space=pl.ANY)
     dma = pltpu.SemaphoreType.DMA
+    swap_scratch = []
+    if trades(inner, narrow):
+        swap_scratch = [pltpu.VMEM((held, HALF, BLK), dens.dtype)] * HALVES
+        swap_scratch += [dma((HALVES,)), dma((HALVES,))]
     return pl.pallas_call(
         functools.partial(step_kernel, steps, inner, narrow, row_cap, col_cap, far_scale),
         out_shape=jax.ShapeDtypeStruct(dens.shape, jnp.float32),
@@ -615,6 +718,7 @@
         out_specs=anywhere,
         scratch_shapes=[pltpu.VMEM((held, HALF, BLK), dens.dtype)] * (steps * HALVES)
         + [pltpu.VMEM((group * cap + 1, HALF, BLK), dens.dtype)] * (steps * HALVES)
+        + swap_scratch
         + [
             pltpu.VMEM((2, HALVES, group, cap, HALF, BLK), dens.dtype),
             pltpu.SMEM(block_slot.shape, ints),
@@ -676,7 +780,7 @@
     return whole_step(
         block_slot,
         region_blocks,
-        basis_lists,
+        basis_lists.T,
         point_counts,
         weights,
         density,

time: 216 us -> 210 us (0.972)
  Pallas kernels: 211 us -> 207 us
    pallas_call x1, Pallas kernels: 211 us -> 207 us  [whole_step(): pl.pallas_call(functools.partial(step_kernel, steps, inner, narrow, row_c...]
    unnamed x2 -> x1, local copies, waits for them, and re-layouts: 4.52 us -> 3.16 us
where the time goes in v3:
time: 210 us
  Pallas kernels  207 us (99%)
  local copies, waits for them, and re-layouts  3.16 us (2%)
    pallas_call x1, Pallas kernels, whole_step(): pl.pallas_call(functools.partial(step_kernel, steps, inner, narrow, row_c...  207 us

profile of v3, /device:TPU:0, one launch (start us, length us, event | category | flops | bytes accessed | tf_op | source)
XLA Modules:
  0.0 210.2 jit_solution(7495662167693000938)
XLA Ops:
  0.0 207.1 %grid_step.1 = f32[512,1024]{1,0:T(8,128)} custom-call(s32[32]{0:T(128)} %slot_ref.1, s32[16]{0:T(128)} %region_ref.1, s32[8,12]{1,0:T(8,128)} %bitcast.3, s32[12]{0:T(128)} %counts_ref.1, f32[12,256]{1,0:T(8,128)} %weights_ref.1, bf16[512,1024]{1,0:T(8,128)(2,1)} %dens_ref.1, bf16[12,8,128,256]{3,2,1,0:T(8,128)(2,1)} %bitcast.2, bf16[12,64,256]{2,1,0:T(8,128)(2,1)} %harm_ref.1), custom_call_target="tpu_custom_call" | custom-call | tf_op jit(solution)/shard_map/grid_step/pallas_call | solution.py:714
  207.1 3.2 %copy.10 = f32[512,1024]{1,0:T(8,128)} copy(f32[512,1024]{1,0:T(8,128)} %grid_step.1) | data formatting | bytes 4194304

commit v4 on v3

--- a/solution.py
+++ b/solution.py
@@ -550,7 +550,7 @@
         potential = 0.5 * dens - sixth + far / far_scale
         factor[:, across] = jnp.broadcast_to(live_row(batch) * potential, (8, points))
 
-    def scale_rows(step, across):
+    def scale_rows(step, across, where):
         ring = lax.rem(ring_me - 1 - step + 2 * steps, steps)
         owner = (ring * inner + across) * row_cap
         spots = [table[mine, 4, owner + rr] for rr in range(row_cap)]
@@ -560,15 +560,15 @@
             for rr in range(row_cap):
                 mate = phi[spots[rr], :, span]
                 scaled = mate.astype(jnp.float32) * factor[0:1, span]
-                rows[rr * BLK : (rr + 1) * BLK, span] = scaled.astype(rows.dtype)
+                rows[where, rr * BLK : (rr + 1) * BLK, span] = scaled.astype(rows.dtype)
             return carry
 
-        lax.fori_loop(0, all_points // CHUNK, chunk, 0)
-
-    def integral_piece(along, put):
+        lax.fori_loop(0, all_points // CHUNK, chunk, 0, unroll=True)
+
+    def integral_piece(along, where, put):
         down = pl.ds(along * col_cap, col_cap)
         term = lax.dot_general(
-            rows[...],
+            rows[where],
             phi[down].reshape(broad, all_points),
             (((1,), (1,)), ((), ())),
             preferred_element_type=jnp.float32,
@@ -583,35 +583,57 @@
             for half in both:
                 over_blocks(step - 2, half, wait_send, plain=True)
 
-        def piece(place):
+        def piece(place, where):
             _, along = target(place)
 
             def put(index, value):
                 for half in both:
                     chosen[step % 2, half, place, index] = value[half * HALF : (half + 1) * HALF]
 
-            integral_piece(along, put)
+            integral_piece(along, where, put)
+
+        def far_rows(count, carry):
+            shift = inner - 1 - count
+
+            @pl.when(count > 0)
+            def _():
+                scale_rows(step, lax.rem(inner_me + shift, inner), 0)
+
+            def body(index, inner_carry):
+                place = shift * narrow + narrow - 1 - index
+
+                @pl.when(place < group - 1)
+                def _():
+                    piece(place, 0)
+
+                @pl.when(place < group - 2)
+                def _():
+                    block_copy(step, 0, place + 1).start()
+
+                return inner_carry
+
+            lax.fori_loop(0, narrow, body, 0)
+            return carry
+
+        scale_rows(step, lax.rem(inner_me + inner - 1, inner), 0)
+        piece(group - 1, 0)
+        if inner > 1:
+            scale_rows(step, inner_me, 1)
+        block_copy(step, 0, group - 1).start()
+        lax.fori_loop(0, inner - 1, far_rows, 0)
+        home = 1 if inner > 1 else 0
+
+        def near(index, carry):
+            place = narrow - 1 - index
 
             @pl.when(place < group - 1)
             def _():
+                piece(place, home)
+
+            @pl.when(place < group - 2)
+            def _():
                 block_copy(step, 0, place + 1).start()
 
-        def far_rows(count, carry):
-            shift = inner - 1 - count
-            scale_rows(step, lax.rem(inner_me + shift, inner))
-
-            def body(index, inner_carry):
-                piece(shift * narrow + narrow - 1 - index)
-                return inner_carry
-
-            lax.fori_loop(0, narrow, body, 0)
-            return carry
-
-        lax.fori_loop(0, inner - 1, far_rows, 0)
-        scale_rows(step, inner_me)
-
-        def near(index, carry):
-            piece(narrow - 1 - index)
             return carry
 
         lax.fori_loop(0, narrow - 1, near, 0)
@@ -620,8 +642,9 @@
             for half in both:
                 arrs[step][half][mine * cap + index] = value[half * HALF : (half + 1) * HALF]
 
-        integral_piece(narrow_me, put_own)
-        block_copy(step, 0, 1).start()
+        integral_piece(narrow_me, home, put_own)
+        if group > 2:
+            block_copy(step, 0, 1).start()
 
         def later(count, carry):
             block_copy(step, 1, group - 1 - count).start()
@@ -735,7 +758,7 @@
             pltpu.VMEM((list_len + 1, BLK, points), orbitals.dtype),
             pltpu.VMEM((list_len + 1, BLK, points), orbitals.dtype),
             pltpu.VMEM((slots + 1, BLK, all_points), orbitals.dtype),
-            pltpu.VMEM((row_cap * BLK, all_points), orbitals.dtype),
+            pltpu.VMEM((2, row_cap * BLK, all_points), orbitals.dtype),
             pltpu.VMEM(harmonics.shape, harmonics.dtype),
             pltpu.VMEM((8, all_points), jnp.float32),
             pltpu.VMEM((8, all_points), jnp.float32),
@@ -763,6 +786,42 @@
     )(block_slot, region_blocks, lists, counts, weights, dens, orbitals, harmonics)
 
 
+def settle_kernel(given_ref, out_ref, held, sems):
+    chunks, size = held.shape[0], held.shape[1]
+
+    def copy(index, out):
+        span = pl.ds(index * size, size)
+        if out:
+            return pltpu.make_async_copy(held.at[index], out_ref.at[span], sems.at[1, index])
+        return pltpu.make_async_copy(given_ref.at[span], held.at[index], sems.at[0, index])
+
+    for index in range(chunks):
+        copy(index, False).start()
+    for index in range(chunks):
+        copy(index, False).wait()
+        copy(index, True).start()
+    for index in range(chunks):
+        copy(index, True).wait()
+
+
+def settle(result):
+    chunks = 8
+    rows, cols = result.shape
+    anywhere = pl.BlockSpec(memory_space=pl.ANY)
+    return pl.pallas_call(
+        settle_kernel,
+        out_shape=jax.ShapeDtypeStruct(result.shape, result.dtype),
+        in_specs=[anywhere],
+        out_specs=anywhere,
+        scratch_shapes=[
+            pltpu.VMEM((chunks, rows // chunks, cols), result.dtype),
+            pltpu.SemaphoreType.DMA((2, chunks)),
+        ],
+        compiler_params=pltpu.CompilerParams(vmem_limit_bytes=VMEM_BYTES),
+        name="settle",
+    )(result)
+
+
 def per_device(
     region, density, block_slot, region_blocks, basis_lists, point_counts, orbitals, weights, harmonics
 ):
@@ -777,7 +836,7 @@
     components = harmonics.shape[1]
     batches, _, points = orbitals.shape
     total_points = batches * points * devices
-    return whole_step(
+    result = whole_step(
         block_slot,
         region_blocks,
         basis_lists.T,
@@ -792,6 +851,7 @@
         (row_cap, col_cap),
         math.sqrt(total_points * components),
     )
+    return settle(result)
 
 
 def solution(mesh):

time: 210 us -> 209 us (level)
  local copies, waits for them, and re-layouts: 3.16 us -> 0 us
    unnamed x1 -> x0, local copies, waits for them, and re-layouts: 3.16 us -> none
    pallas_call x0 -> x1, Pallas kernels: none -> 2.4 us  [settle(): pl.pallas_call(settle_kernel, out_shape=jax.ShapeDtypeStruct(result.shape...]
where the time goes in v4:
time: 209 us
  Pallas kernels  209 us (100%)
    pallas_call x1, Pallas kernels, whole_step(): pl.pallas_call(functools.partial(step_kernel, steps, inner, narrow, row_c...  206 us

profile of v4, /device:TPU:0, one launch (start us, length us, event | category | flops | bytes accessed | tf_op | source)
XLA Modules:
  0.0 208.8 jit_solution(284706107242496642)
XLA Ops:
  0.0 206.2 %grid_step.1.given_ref = f32[512,1024]{1,0:T(8,128)} custom-call(s32[32]{0:T(128)} %slot_ref.1, s32[16]{0:T(128)} %region_ref.1, s32[8,12]{1,0:T(8,128)} %bitcast.3, s32[12]{0:T(128)} %counts_ref.1, f32[12,256]{1,0:T(8,128)} %weights_ref.1, bf16[512,1024]{1,0:T(8,128)(2,1)} %dens_ref.1, bf16[12,8,128,256]{3,2,1,0:T(8,128)(2,1)} %bitcast.2, ...), custom_call_target="tpu_custom_call" | custom-call | tf_op jit(solution)/shard_map/grid_step/pallas_call | solution.py:737
  206.2 2.4 %settle.1 = f32[512,1024]{1,0:T(8,128)} custom-call(f32[512,1024]{1,0:T(8,128)} %grid_step.1.given_ref), custom_call_target="tpu_custom_call" | custom-call | tf_op jit(solution)/shard_map/settle/pallas_call | solution.py:811

commit v5 on v4

--- a/solution.py
+++ b/solution.py
@@ -321,6 +321,11 @@
             if step < steps - 1:
                 ring_copy(step, half, piece).start()
 
+    def sent_on():
+        for step in range(steps - 1):
+            for half in range(HALVES):
+                over(0, row_blocks, functools.partial(ring_copy, step, half), wait_send)
+
     def pick(step, half, place, put):
         across, along = target(place)
         other = across * narrow + along
@@ -500,7 +505,12 @@
         send_picks(step, 1)
         density_pieces(step - 1, both, middle, group - 1)
         density_piece(step - 1, both, 0)
+    if square:
+        for half in both:
+            swap_copy(half).wait_send()
     for half in both:
+        if half == 1:
+            sent_on()
         density_piece(steps - 1, (half,), 0)
         density_pieces(steps - 1, (half,), 0, group - 1)
 
@@ -528,15 +538,10 @@
     share[...] = jnp.broadcast_to(line, share.shape)
     whose, _ = any_device(0)
     shares[whose] = jnp.broadcast_to(line, share.shape)
+    over(1, devices, share_copy, start)
     for half in both:
-        for step in range(steps - 1):
-            over(0, row_blocks, functools.partial(ring_copy, step, half), wait_send)
         for step in range(max(0, steps - 2), steps):
             over_blocks(step, half, wait_send)
-    if square:
-        for half in both:
-            swap_copy(half).wait_send()
-    over(1, devices, share_copy, start)
     over(1, devices, share_copy, wait)
     line = jnp.sum(shares[...], axis=0)[0:1]
     total_moment = jnp.sum(jnp.where(diagonal, line, 0.0), axis=1, keepdims=True)
@@ -655,7 +660,7 @@
     def out_copy(half, piece):
         first = pl.multiple_of(piece * BLK + half * HALF, HALF)
         return pltpu.make_async_copy(
-            ostage.at[piece % 2], out_ref.at[pl.ds(first, HALF)], out_sem.at[piece % 2]
+            ostage.at[piece], out_ref.at[pl.ds(first, HALF)], out_sem.at[piece]
         )
 
     def add_up(step, half):
@@ -665,8 +670,6 @@
         for piece in range(row_blocks):
             if step > 0:
                 ring_copy(step - 1, half, piece).wait_recv()
-            if last and piece >= 2:
-                out_copy(half, piece - 2).wait()
             bases = [
                 table[one, 2, (ring * inner + inner_me) * row_blocks + piece] + one * cap
                 for one in range(group)
@@ -684,7 +687,7 @@
                     total += arrs[step][half][place].astype(jnp.float32)
                 if last:
                     across = pl.ds(pl.multiple_of(block * BLK, BLK), BLK)
-                    ostage[piece % 2, :, across] = total
+                    ostage[piece, :, across] = total
                 else:
                     raws[step][half][spot] = total.astype(chosen.dtype)
                 return carry
@@ -697,7 +700,9 @@
         if not last:
             ring_copy(step, half, row_blocks - 1).start()
         else:
-            for piece in range(max(0, row_blocks - 2), row_blocks):
+            if half == 1:
+                over_blocks(step, half, wait_send, plain=True)
+            for piece in range(row_blocks):
                 out_copy(half, piece).wait()
 
     send_integrals(0)
@@ -705,12 +710,13 @@
         add_up(step, 0)
         if step + 1 < steps:
             send_integrals(step + 1)
+        else:
+            sent_on()
+            if steps > 1:
+                for half in both:
+                    over_blocks(step - 1, half, wait_send, plain=True)
+            over_blocks(step, 0, wait_send, plain=True)
         add_up(step, 1)
-    for half in both:
-        for step in range(max(0, steps - 2), steps):
-            over(1, group, functools.partial(block_copy, step, half), wait_send)
-        for step in range(steps - 1):
-            over(0, row_blocks, functools.partial(ring_copy, step, half), wait_send)
 
 
 def whole_step(
@@ -764,7 +770,7 @@
             pltpu.VMEM((8, all_points), jnp.float32),
             pltpu.VMEM((8, LANES), jnp.float32),
             pltpu.VMEM((devices, 8, LANES), jnp.float32),
-            pltpu.VMEM((2, HALF, dens.shape[1]), jnp.float32),
+            pltpu.VMEM((row_blocks, HALF, dens.shape[1]), jnp.float32),
             dma((steps, HALVES, group)),
             dma((steps, HALVES, group)),
             dma((ring_sems, HALVES, row_blocks)),
@@ -777,7 +783,7 @@
             dma((4,)),
             dma((devices,)),
             dma((devices,)),
-            dma((2,)),
+            dma((row_blocks,)),
         ],
         compiler_params=pltpu.CompilerParams(
             collective_id=1, has_side_effects=True, vmem_limit_bytes=VMEM_BYTES

time: 209 us -> 208 us (level)
  no operation moved by 1% of the time
where the time goes in v5:
time: 208 us
  Pallas kernels  208 us (100%)
    pallas_call x1, Pallas kernels, whole_step(): pl.pallas_call(functools.partial(step_kernel, steps, inner, narrow, row_c...  205 us

profile of v5, /device:TPU:0, one launch (start us, length us, event | category | flops | bytes accessed | tf_op | source)
XLA Modules:
  0.0 207.8 jit_solution(7983162558050606729)
XLA Ops:
  0.0 205.2 %grid_step.1.given_ref = f32[512,1024]{1,0:T(8,128)} custom-call(s32[32]{0:T(128)} %slot_ref.1, s32[16]{0:T(128)} %region_ref.1, s32[8,12]{1,0:T(8,128)} %bitcast.3, s32[12]{0:T(128)} %counts_ref.1, f32[12,256]{1,0:T(8,128)} %weights_ref.1, bf16[512,1024]{1,0:T(8,128)(2,1)} %dens_ref.1, bf16[12,8,128,256]{3,2,1,0:T(8,128)(2,1)} %bitcast.2, ...), custom_call_target="tpu_custom_call" | custom-call | tf_op jit(solution)/shard_map/grid_step/pallas_call | solution.py:743
  205.2 2.4 %settle.1 = f32[512,1024]{1,0:T(8,128)} custom-call(f32[512,1024]{1,0:T(8,128)} %grid_step.1.given_ref), custom_call_target="tpu_custom_call" | custom-call | tf_op jit(solution)/shard_map/settle/pallas_call | solution.py:817
